TPU v7x, 512 devices: a whole 4x4x16 slice. The times are simulated.
512 devices in a mesh: row: 16 (over z_hi, y, core), col: 32 (over z_lo, x).
Axes of the slice: x: 4, y: 4, z: 16 (z_hi: 2, z_lo: 8; z = z_hi * 8 + z_lo), core: 2. Of those that a mesh axis runs over, the one named last changes fastest.
Arguments:
- query_grads: bfloat16 [256, 8192], P('row', 'col'), may hold values from -6 to 6
- query_acts: bfloat16 [256, 8192], P('col', 'row'), may hold values from -6 to 6
- train_grads: bfloat16 [512, 8192], P('row', 'col'), may hold values from -6 to 6
- train_acts: bfloat16 [512, 8192], P('col', 'row'), may hold values from -6 to 6
- grad_basis: bfloat16 [8192, 8192], P('col', 'row'), may hold values from -0.0625 to 0.0625
- act_basis: bfloat16 [8192, 8192], P('row', 'col'), may hold values from -0.0625 to 0.0625
- eigen_corr: float32 [8192, 8192], P('row', 'col'), may hold values from 0.02 to 2
- damping: float32 [], replicated, may hold values from 0.05 to 0.5
- query_seq: int32 [256], replicated, may hold values from 0 to 31, never falling along the last dimension, each value on 1 to 16 neighbouring positions
- train_doc: int32 [512], replicated, may hold values from 0 to 15, never falling along the last dimension, each value on 1 to 64 neighbouring positions
Outputs:
- scores: float32 [32, 512], P(None, 'col')
- doc_scores: float32 [32, 16], replicated
Inputs may be any that keep to these rules, and one draw needn't show every extreme that they name: `query_seq`: Non-decreasing along the query tokens; every sequence has 1 to 16 tokens, and one has exactly that many. `train_doc`: Non-decreasing along the training tokens; every document has 1 to 64 tokens, and one has exactly that many.
All inputs are finite; a program needn't handle non-finite values.
Results may differ from a plain program's by a relative error of at most 0.005.
Values may be sent and summed in bfloat16 or wider, within the bound.
No kernel may reach another device: no remote copies, remote signals or barrier semaphores. Data moves between devices by JAX's collectives and lax.ppermute only.
A program may use at most 64 MiB of HBM per device.

v0:
```python
import jax
import jax.numpy as jnp
from jax import lax
from jax.sharding import PartitionSpec as P

D = 8192
S = 32
DOCS = 16


def local(
    query_grads,
    query_acts,
    train_grads,
    train_acts,
    grad_basis,
    act_basis,
    eigen_corr,
    damping,
    query_seq,
    train_doc,
):
    grad_query, grad_train = (
        lax.all_gather(query_grads, "row", axis=0, tiled=True),
        lax.all_gather(train_grads, "row", axis=0, tiled=True),
    )
    act_query, act_train = (
        lax.all_gather(query_acts, "col", axis=0, tiled=True),
        lax.all_gather(train_acts, "col", axis=0, tiled=True),
    )
    grads_all = jnp.concatenate([grad_query, grad_train], axis=0)
    acts_all = jnp.concatenate([act_query, act_train], axis=0)
    n_query = grad_query.shape[0]
    grad_part = jnp.dot(grads_all, grad_basis, preferred_element_type=jnp.float32)
    grads_rot = lax.psum(grad_part, "col").astype(jnp.bfloat16)
    act_part = jnp.dot(acts_all, act_basis, preferred_element_type=jnp.float32)
    acts_rot = lax.psum(act_part, "row").astype(jnp.bfloat16)
    rot_gq = grads_rot[:n_query]
    rot_gu = grads_rot[n_query:]
    rot_aq = acts_rot[:n_query]
    rot_au = acts_rot[n_query:]
    denom = eigen_corr + damping
    act_wide = rot_au.astype(jnp.float32)
    row_block = eigen_corr.shape[0]
    col_block = eigen_corr.shape[1]
    group = 4

    def score_group(first):
        seq_ids = first + jnp.arange(group, dtype=jnp.int32)
        member = (query_seq[:, None] == seq_ids[None, :]).astype(jnp.bfloat16)
        weighted = (member[:, :, None] * rot_gq[:, None, :]).reshape(n_query, group * row_block)
        outer = lax.dot_general(
            weighted, rot_aq, (((0,), (0,)), ((), ())), preferred_element_type=jnp.float32
        )
        precond = (outer.reshape(group, row_block, col_block) / denom[None, :, :]).astype(
            jnp.bfloat16
        )
        mapped = jnp.einsum("ui,sij->usj", rot_gu, precond, preferred_element_type=jnp.float32)
        return jnp.sum(mapped * act_wide[:, None, :], axis=2).T

    starts = jnp.arange(S // group, dtype=jnp.int32) * group
    partial_scores = lax.map(score_group, starts).reshape(S, rot_gu.shape[0]) / D
    doc_table = (train_doc[:, None] == jnp.arange(DOCS, dtype=jnp.int32)[None, :]).astype(
        jnp.float32
    )
    counts = jnp.sum(doc_table, axis=0)
    owned = rot_gu.shape[0] // lax.axis_size("col")
    first_owned = lax.axis_index("col") * owned
    totals = lax.psum(partial_scores, ("row", "col"))
    scores = lax.dynamic_slice_in_dim(totals, first_owned, owned, 1)
    doc_sum = jnp.dot(totals, doc_table, precision=lax.Precision.HIGHEST)
    return (scores, doc_sum / counts[None, :])


def solution(mesh):
    in_specs = (
        P("row", "col"),
        P("col", "row"),
        P("row", "col"),
        P("col", "row"),
        P("col", "row"),
        P("row", "col"),
        P("row", "col"),
        P(),
        P(),
        P(),
    )
    out_specs = (P(None, "col"), P())
    return jax.shard_map(local, mesh=mesh, in_specs=in_specs, out_specs=out_specs, check_vma=False)
```

profile of v0, /device:TPU:1, one launch (start us, length us, event | category | flops | bytes accessed | tf_op | source)
XLA Modules:
  0.0 1171.2 jit_solution(7079369166472949300)
XLA Ops:
  7.2 52.0 %all_gather.13 = bf16[512,256]{1,0:T(8,128)(2,1)S(1)} all-gather(bf16[32,256]{1,0:T(8,128)(2,1)} %param.14), channel_id=1, replica_groups=mesh['row'=16,'col'=32] {'row'}, dimensions={0}, use_global_device_ids=true | all-gather | bytes 278528 | tf_op jit(solution)/shard_map/all_gather | solution.py:25
  59.2 34.3 %all_gather.12 = bf16[256,256]{1,0:T(8,128)(2,1)S(1)} all-gather(bf16[16,256]{1,0:T(8,128)(2,1)} %param.12), channel_id=1, replica_groups=mesh['row'=16,'col'=32] {'row'}, dimensions={0}, use_global_device_ids=true | all-gather | bytes 139264 | tf_op jit(solution)/shard_map/all_gather | solution.py:24
  93.9 219.5 %all-reduce.5 = bf16[768,512]{1,0:T(8,128)(2,1)S(1)} all-reduce(f32[768,512]{1,0:T(8,128)S(1)} %fusion.16), channel_id=1, replica_groups=mesh['row'=16,'col'=32] {'col'}, use_global_device_ids=true, to_apply=%region_0.0 | all-reduce | flops 393216 | bytes 2359296 | tf_op jit(solution)/shard_map/psum | solution.py:35
  313.4 100.8 %all_gather.15 = bf16[512,512]{1,0:T(8,128)(2,1)S(1)} all-gather(bf16[16,512]{1,0:T(8,128)(2,1)S(1)} %copy-done.4), channel_id=1, replica_groups=mesh['row'=16,'col'=32] {'col'}, dimensions={0}, use_global_device_ids=true | all-gather | bytes 540672 | tf_op jit(solution)/shard_map/all_gather | solution.py:29
  414.2 100.0 %all_gather.14 = bf16[256,512]{1,0:T(8,128)(2,1)S(1)} all-gather(bf16[8,512]{1,0:T(8,128)(2,1)S(1)} %copy-done.5), channel_id=1, replica_groups=mesh['row'=16,'col'=32] {'col'}, dimensions={0}, use_global_device_ids=true | all-gather | bytes 270336 | tf_op jit(solution)/shard_map/all_gather | solution.py:28
  514.6 176.3 %all-reduce.6 = bf16[768,256]{1,0:T(8,128)(2,1)S(1)} all-reduce(f32[768,256]{1,0:T(8,128)S(1)} %fusion.12), channel_id=1, replica_groups=mesh['row'=16,'col'=32] {'row'}, use_global_device_ids=true, to_apply=%region_1.0 | all-reduce | flops 196608 | bytes 1179648 | tf_op jit(solution)/shard_map/psum | solution.py:37
  692.1 19.3 %while.10 = (s32[]{:T(128)}, f32[8,4,512]{2,1,0:T(4,128)S(1)}, s32[256]{0:T(256)S(1)}, s32[8]{0:T(128)S(1)}, bf16[256,512]{0,1:T(8,128)(2,1)S(1)}, /*index=5*/bf...) while((s32[]{:T(128)}, f32[8,4,512]{2,1,0:T(4,128)S(1)}, ...), condition=%wide.region_4.5_spmd, body=%wide.region_2.4_spmd.sunk | while | flops 807927808 | bytes 1995929 | solution.py:62
  692.7 0.6 iota_add_fusion.2
  693.4 1.1 fusion.33
  694.5 0.6 dynamic_slice.10
  695.1 0.6 iota_add_fusion.2
  695.8 1.1 fusion.33
  696.9 0.6 dynamic_slice.10
  697.5 0.6 iota_add_fusion.2
  698.2 1.1 fusion.33
  699.3 0.6 dynamic_slice.10
  699.9 0.6 iota_add_fusion.2
  700.7 1.1 fusion.33
  702.4 0.6 iota_add_fusion.2
  703.1 1.1 fusion.33
  704.8 0.6 iota_add_fusion.2
  705.5 1.1 fusion.33
  706.6 0.6 dynamic_slice.10
  707.2 0.6 iota_add_fusion.2
  707.9 1.1 fusion.33
  709.6 0.6 iota_add_fusion.2
  710.3 1.1 fusion.33
  711.5 0.6 div.26
  712.2 449.1 %all-reduce.4.cloned.1.call-done = f32[32,512]{1,0:T(8,128)} async-done(((f32[32,512]{1,0:T(8,128)}), f32[32,512]{1,0:T(8,128)}) %all-reduce.4.cloned.1.call-update) | async-done | bytes 65552 | tf_op jit(solution)/shard_map/psum | solution.py:69
  1161.3 0.8 constant_dynamic-slice_fusion
  1162.1 0.7 copy.21
  1162.8 1.6 convolution_divide_fusion
  (52 shorter events, 4.5 us)
Async XLA Ops:
  7.2 86.4 %copy-start = (bf16[256,512]{1,0:T(8,128)(2,1)S(1)}, bf16[256,512]{1,0:T(8,128)(2,1)}, u32[]{:S(2)}) copy-start(bf16[256,512]{1,0:T(8,128)(2,1)} %param.16) | copy-start | bytes 786436
  7.2 1154.2 %all-reduce.4.cloned.1.call-start = ((), (), s32[]{:S(2)}) async-start(), calls=%async_computation | async-start | bytes 131072 | tf_op jit(solution)/shard_map/psum | solution.py:69
  93.9 219.6 %copy-start.4 = (bf16[16,512]{1,0:T(8,128)(2,1)S(1)}, bf16[16,512]{1,0:T(8,128)(2,1)}, u32[]{:S(2)}) copy-start(bf16[16,512]{1,0:T(8,128)(2,1)} %param.15) | copy-start | bytes 49156
  313.4 201.2 %copy-start.1 = (bf16[768,512]{1,0:T(8,128)(2,1)}, bf16[768,512]{1,0:T(8,128)(2,1)S(1)}, u32[]{:S(2)}) copy-start(bf16[768,512]{1,0:T(8,128)(2,1)S(1)} %all-reduce.5) | copy-start | bytes 2359300
  313.4 100.8 %copy-start.5 = (bf16[8,512]{1,0:T(8,128)(2,1)S(1)}, bf16[8,512]{1,0:T(8,128)(2,1)}, u32[]{:S(2)}) copy-start(bf16[8,512]{1,0:T(8,128)(2,1)} %param.13) | copy-start | bytes 24580
  313.4 200.8 %copy-start.7 = (bf16[512,256]{1,0:T(8,128)(2,1)S(1)}, bf16[512,256]{1,0:T(8,128)(2,1)}, u32[]{:S(2)}) copy-start(bf16[512,256]{1,0:T(8,128)(2,1)} %param.17) | copy-start | bytes 786436
  690.9 1.1 copy-start.2
  690.9 1.2 slice-start
  690.9 1.2 copy-start.3
  692.1 20.0 %copy-start.6 = (s32[512]{0:T(512)S(1)}, s32[512]{0:T(512)}, u32[]{:S(2)}) copy-start(s32[512]{0:T(512)} %param.21) | copy-start | bytes 6148
Sparse Core Ops, SparseCore 0:
  712.2 449.0 all-reduce.3
where the time goes:
time: 1170 us
  blocking collectives  683 us (58%)
  waiting for transfers between devices  449 us (38%)
  between operations  14.9 us (1%)
    psum x1, waiting for transfers between devices, local(): totals = lax.psum(partial_scores, ('row', 'col'))  449 us
    psum x1, blocking collectives, local(): grads_rot = lax.psum(grad_part, 'col').astype(jnp.bfloat16)  219 us
    psum x1, blocking collectives, local(): acts_rot = lax.psum(act_part, 'row').astype(jnp.bfloat16)  176 us
    all_gather x1, blocking collectives, local(): lax.all_gather(train_acts, 'col', axis=0, tiled=True)  101 us
    all_gather x1, blocking collectives, local(): lax.all_gather(query_acts, 'col', axis=0, tiled=True)  100 us
    all_gather x1, blocking collectives, local(): lax.all_gather(train_grads, 'row', axis=0, tiled=True)  52 us
    all_gather x1, blocking collectives, local(): lax.all_gather(query_grads, 'row', axis=0, tiled=True)  34.3 us
  transfers between devices with their start and end apart: 1, of which 1 were waited for; matrix products, arithmetic and copies ran while one was open for 0% of the time, Pallas kernels for 0%

commit v1 on v0

v1 whole, which is shorter than its diff:
```python
import jax
import jax.numpy as jnp
from jax import lax
from jax.sharding import Mesh, PartitionSpec as P


D = 8192
S = 32
DOCS = 16
ROW = ("zh", "y", "c")
COL = ("zl", "x")


def spread(v, axes):
    n = lax.axis_size(axes)
    return lax.all_to_all(jnp.broadcast_to(v[None], (n,) + v.shape), axes, 0, 0, tiled=True)


def exchange(parts, axes):
    return lax.all_to_all(parts, axes, 0, 0, tiled=True)


def split(v):
    hi = lax.reduce_precision(v, 8, 7)
    return hi.astype(jnp.bfloat16), (v - hi).astype(jnp.bfloat16)


def shift(v, axis, k):
    n = lax.axis_size(axis)
    return lax.ppermute(v, axis, [(i, (i + k) % n) for i in range(n)])


def around(v, axis):
    n = lax.axis_size(axis)
    return jnp.stack([v] + [shift(v, axis, n - k) for k in range(1, n)])


def turn(v, axis):
    n = lax.axis_size(axis)
    return lax.dynamic_slice_in_dim(
        jnp.concatenate([v, v[: n - 1]], axis=0), (n - lax.axis_index(axis)) % n, n, 0
    )


def body(
    query_grads,
    query_acts,
    train_grads,
    train_acts,
    grad_basis,
    act_basis,
    eigen_corr,
    damping,
    query_seq,
    train_doc,
):
    bf16, f32 = jnp.bfloat16, jnp.float32
    n_query, n_train = query_seq.shape[0], train_doc.shape[0]
    nx, nzl, nzh = lax.axis_size("x"), lax.axis_size("zl"), lax.axis_size("zh")
    nyc = lax.axis_size(("y", "c"))
    q, t = query_acts.shape[0], train_acts.shape[0]
    n = q + t
    fi, fj = eigen_corr.shape

    a = spread(jnp.concatenate([query_acts, train_acts], axis=0), "zl")
    a = spread(a, "x")
    act_part = jnp.dot(a.reshape(-1, a.shape[-1]), act_basis, preferred_element_type=f32)
    act_part = act_part.astype(bf16).reshape(nyc, -1, fj)
    a = exchange(act_part, ("y", "c"))
    a = jnp.sum(a.astype(f32), axis=0)
    a = (a + lax.ppermute(a, "zh", [(0, 1), (1, 0)])).astype(bf16)
    a = around(a, "y")
    a = lax.all_gather(a, "c")
    acts = turn(jnp.swapaxes(a, 0, 1), "y").reshape(nx, nzl, n, fj)

    g = jnp.concatenate(
        [query_grads[:q], train_grads[:t], query_grads[q:], train_grads[t:]], axis=0
    )
    other = lax.ppermute(g, "zh", [(0, 1), (1, 0)])
    first = lax.axis_index("zh") == 0
    g = jnp.concatenate([jnp.where(first, g, other), jnp.where(first, other, g)], axis=0)
    g = around(g, "y")
    g = lax.all_gather(g, "c")
    g = g.reshape(n_query + n_train, -1)
    grad_part = jnp.dot(g, grad_basis, preferred_element_type=f32)
    grad_part = grad_part.astype(bf16).reshape(nx, -1, fi)
    x = lax.axis_index("x")
    own = [lax.dynamic_index_in_dim(grad_part, (x + k) % nx, 0, False) for k in range(nx)]
    got = [own[0]] + [shift(own[k], "x", k) for k in (1, nx - 1, 2)]
    g = sum(v.astype(f32) for v in got)
    g_hi, g_lo = split(g.reshape(nzl, n, fi))
    g = exchange(jnp.concatenate([g_hi, g_lo[:, :q]], axis=1), "zl").astype(f32)
    g = jnp.sum(g, axis=0)
    g = jnp.concatenate([g[:q] + g[n:], g[q:n]], axis=0).astype(bf16)
    g = spread(g, "zl").reshape(-1, fi)
    g = spread(g, "x")
    g = g.reshape(2, -1, nzh, 2, n, fi)
    grads = turn(jnp.moveaxis(g, 0, 2), "y")
    grads = jnp.swapaxes(grads, 0, 1)

    acts = jnp.swapaxes(acts, 0, 1)
    rot_gq = grads[..., :q, :].reshape(n_query, fi)
    rot_gu = grads[..., q:, :].reshape(n_train, fi)
    rot_aq = acts[:, :, :q].reshape(n_query, fj)
    rot_au = acts[:, :, q:].reshape(n_train, fj)
    denom = eigen_corr + damping
    act_wide = rot_au.astype(f32)
    group = 4

    def score_group(first):
        seq_ids = first + jnp.arange(group, dtype=jnp.int32)
        member = (query_seq[:, None] == seq_ids[None, :]).astype(bf16)
        weighted = (member[:, :, None] * rot_gq[:, None, :]).reshape(n_query, group * fi)
        outer = lax.dot_general(
            weighted, rot_aq, (((0,), (0,)), ((), ())), preferred_element_type=f32
        )
        precond = (outer.reshape(group, fi, fj) / denom[None, :, :]).astype(bf16)
        mapped = jnp.einsum("ui,sij->usj", rot_gu, precond, preferred_element_type=f32)
        return jnp.sum(mapped * act_wide[:, None, :], axis=2).T

    starts = jnp.arange(S // group, dtype=jnp.int32) * group
    partial_scores = lax.map(score_group, starts).reshape(S, n_train) / D
    doc_table = (train_doc[:, None] == jnp.arange(DOCS, dtype=jnp.int32)[None, :]).astype(f32)
    counts = jnp.sum(doc_table, axis=0)
    doc_part = jnp.dot(partial_scores, doc_table, precision=lax.Precision.HIGHEST)

    lanes = nzl * t
    p = partial_scores.reshape(S, nzl, nx, t)
    p = jnp.moveaxis(p, 2, 0).reshape(nx, S, lanes)
    d = jnp.broadcast_to(doc_part.reshape(1, -1, lanes), (nx, S * DOCS // lanes, lanes))
    p = jnp.concatenate([p, d, jnp.zeros_like(d)], axis=1)
    p = jnp.broadcast_to(p[None], (nyc,) + p.shape).reshape((nyc * nx,) + p.shape[1:])
    p = jnp.sum(exchange(p, ("y", "c", "x")), axis=0)
    d = p[S : S + S * DOCS // lanes].reshape(S, DOCS)
    p = jnp.swapaxes(p[:S].reshape(S, nzl, t), 0, 1)
    p = jnp.concatenate([p, jnp.broadcast_to(d[None], (nzl, S, DOCS))], axis=2)
    p = jnp.broadcast_to(p[None], (nzh,) + p.shape).reshape(nzh * nzl, -1, 128)
    p = jnp.sum(exchange(p, ("zh", "zl")), axis=0).reshape(S, t + DOCS)
    return (p[:, :t], p[:, t:] / counts[None, :])


def solution(mesh):
    fine = Mesh(mesh.devices.reshape(2, 4, 2, 8, 4), ROW + COL)
    in_specs = (
        P(ROW, COL),
        P(COL, ROW),
        P(ROW, COL),
        P(COL, ROW),
        P(COL, ROW),
        P(ROW, COL),
        P(ROW, COL),
        P(),
        P(),
        P(),
    )
    out_specs = (P(None, COL), P())
    return jax.shard_map(body, mesh=fine, in_specs=in_specs, out_specs=out_specs, check_vma=False)
```

time: 1170 us -> 234 us (0.20)
  blocking collectives: 683 us -> 30.8 us
  waiting for transfers between devices: 449 us -> 56 us
  starting transfers between devices: 0.04 us -> 109 us
  between operations: 14.9 us -> 1.87 us
    psum x1 -> x0, waiting for transfers between devices: 449 us -> none  [local(): totals = lax.psum(partial_scores, ('row', 'col'))]
    psum x2 -> x0, blocking collectives: 396 us -> none  [the longest x1 219 us: local(): grads_rot = lax.psum(grad_part, 'col').astype(jnp.bfloat16)]
    all_gather x4 -> x2, blocking collectives: 287 us -> 9.53 us  [the longest x1 4.87 us: body(): a = lax.all_gather(a, 'c')]
    all_to_all x0 -> x7, starting transfers between devices: none -> 55.8 us  [the longest x3 35.2 us: exchange(): return lax.all_to_all(parts, axes, 0, 0, tiled=True)]
    ppermute x0 -> x11, starting transfers between devices: none -> 53.6 us  [the longest x9 29.1 us: shift(): return lax.ppermute(v, axis, [(i, (i + k) % n) for i in range(n)])]
    all_to_all x0 -> x7, waiting for transfers between devices: none -> 42.6 us  [the longest x3 29.9 us: exchange(): return lax.all_to_all(parts, axes, 0, 0, tiled=True)]
    all_to_all x0 -> x1, blocking collectives: none -> 21.3 us  [exchange(): return lax.all_to_all(parts, axes, 0, 0, tiled=True)]
    ppermute x0 -> x11, waiting for transfers between devices: none -> 13.3 us  [the longest x9 6.08 us: shift(): return lax.ppermute(v, axis, [(i, (i + k) % n) for i in range(n)])]
  transfers between devices with their start and end apart: 1 -> 18, of which waited for: 1 -> 9; matrix products, arithmetic and copies ran while one was open for 0% -> 2% of each run, Pallas kernels for 0% -> 0%
where the time goes in v1:
time: 234 us; the launch traced here: 232 us
  starting transfers between devices  109 us (47%)
  waiting for transfers between devices  56 us (24%)
  blocking collectives  30.8 us (13%)
  local copies, waits for them, and re-layouts  15.6 us (7%)
  matrix products  10.2 us (4%)
  other arithmetic  8.45 us (4%)
    all_to_all x3, starting transfers between devices, exchange(): return lax.all_to_all(parts, axes, 0, 0, tiled=True)  35.2 us
    all_to_all x3, waiting for transfers between devices, exchange(): return lax.all_to_all(parts, axes, 0, 0, tiled=True)  29.9 us
    ppermute x9, starting transfers between devices, shift(): return lax.ppermute(v, axis, [(i, (i + k) % n) for i in range(n)])  29.1 us
    all_to_all x1, blocking collectives, exchange(): return lax.all_to_all(parts, axes, 0, 0, tiled=True)  21.3 us
    all_to_all x4, starting transfers between devices, spread(): lax.all_to_all(jnp.broadcast_to(v[None], (n,) + v.shape), axes, 0, 0, til...  20.6 us
    ppermute x1, starting transfers between devices, body(): other = lax.ppermute(g, 'zh', [(0, 1), (1, 0)])  16.2 us
    all_to_all x4, waiting for transfers between devices, spread(): lax.all_to_all(jnp.broadcast_to(v[None], (n,) + v.shape), axes, 0, 0, til...  12.8 us
    dot_general x8, matrix products, score_group(): jnp.einsum('ui,sij->usj', rot_gu, precond, preferred_element_type=f32)  8.54 us
  transfers between devices with their start and end apart: 18, of which 9 were waited for; matrix products, arithmetic and copies ran while one was open for 2% of the time, Pallas kernels for 0%

profile of v1, /device:TPU:1, one launch (start us, length us, event | category | flops | bytes accessed | tf_op | source)
XLA Modules:
  0.0 232.5 jit_solution(1099224276336530177)
XLA Ops:
  2.1 16.2 %collective-permute-start = (bf16[48,256]{1,0:T(8,128)(2,1)S(1)}, bf16[48,256]{1,0:T(8,128)(2,1)S(1)}, u32[]{:S(2)}, u32[]{:S(2)}) collective-permute-start(bf16[48,256]{1,0:T(8,128)(2,1)S(1)} %pad_maximum_fusion.5), channel_id=1, source_target_pairs={{0,256},{256,0},{1,257},{257,1},{2,258},{258,2},{3,259},{259,3},{4... | collective-permute-start | bytes 73736 | tf_op jit(solution)/shard_map/ppermute | solution.py:79
  18.4 1.3 collective-permute-done
  19.7 3.2 %collective-permute-start.3 = (bf16[96,256]{1,0:T(8,128)(2,1)S(1)}, bf16[96,256]{1,0:T(8,128)(2,1)S(1)}, u32[]{:S(2)}, u32[]{:S(2)}) collective-permute-start(bf16[96,256]{1,0:T(8,128)(2,1)S(1)} %get-tuple-element.129), channel_id=1, source_target_pairs={{0,64},{64,128},{128,192},{192,0},{1,65},{65,129},{129,193},{193,1... | collective-permute-start | bytes 147464 | tf_op jit(solution)/shard_map/ppermute | solution.py:30
  22.9 4.5 %collective-permute-start.2 = (bf16[96,256]{1,0:T(8,128)(2,1)S(1)}, bf16[96,256]{1,0:T(8,128)(2,1)S(1)}, u32[]{:S(2)}, u32[]{:S(2)}) collective-permute-start(bf16[96,256]{1,0:T(8,128)(2,1)S(1)} %get-tuple-element.129), channel_id=1, source_target_pairs={{0,128},{64,192},{128,0},{192,64},{1,129},{65,193},{129,1},{193,65... | collective-permute-start | bytes 147464 | tf_op jit(solution)/shard_map/ppermute | solution.py:30
  27.5 3.0 %collective-permute-start.1 = (bf16[96,256]{1,0:T(8,128)(2,1)S(1)}, bf16[96,256]{1,0:T(8,128)(2,1)S(1)}, u32[]{:S(2)}, u32[]{:S(2)}) collective-permute-start(bf16[96,256]{1,0:T(8,128)(2,1)S(1)} %get-tuple-element.129), channel_id=1, source_target_pairs={{0,192},{64,0},{128,64},{192,128},{1,193},{65,1},{129,65},{193,129... | collective-permute-start | bytes 147464 | tf_op jit(solution)/shard_map/ppermute | solution.py:30
  31.8 8.8 %all-to-all-start.3 = ((bf16[8,24,512]{2,1,0:T(8,128)(2,1)}), bf16[8,24,512]{2,1,0:T(8,128)(2,1)S(1)}, u32[]{:S(2)}, u32[]{:S(2)}) async-start(bf16[8,24,512]{2,1,0:T(8,128)(2,1)} %broadcast_in_dim.39), calls=%async_computation.3 | async-start | bytes 393216 | tf_op jit(solution)/shard_map/all_to_all | solution.py:16
  40.7 4.7 %all-gather = bf16[8,96,256]{2,1,0:T(8,128)(2,1)S(1)} all-gather(bf16[4,96,256]{2,1,0:T(8,128)(2,1)S(1)} %pad_maximum_fusion.1), channel_id=2, replica_groups=mesh['zh'=2,'y'=4,'c'=2,'zl'=8,'x'=4] {'c'}, dimensions={0}, use_global_device_ids=true | all-gather | bytes 589824 | tf_op jit(solution)/shard_map/all_gather | solution.py:83
  45.8 4.7 %collective-permute-start.6 = (bf16[192,512]{1,0:T(8,128)(2,1)S(1)}, bf16[192,512]{1,0:T(8,128)(2,1)S(1)}, u32[]{:S(2)}, u32[]{:S(2)}) collective-permute-start(bf16[192,512]{1,0:T(8,128)(2,1)S(1)} %get-tuple-element.124), channel_id=1, source_target_pairs={{0,2},{1,3},{2,0},{3,1},{4,6},{5,7},{6,4},{7,5},{8,10},{9,11},{10,... | collective-permute-start | bytes 589832 | tf_op jit(solution)/shard_map/ppermute | solution.py:30
  50.4 2.8 %collective-permute-start.5 = (bf16[192,512]{1,0:T(8,128)(2,1)S(1)}, bf16[192,512]{1,0:T(8,128)(2,1)S(1)}, u32[]{:S(2)}, u32[]{:S(2)}) collective-permute-start(bf16[192,512]{1,0:T(8,128)(2,1)S(1)} %get-tuple-element.125), channel_id=1, source_target_pairs={{0,3},{1,0},{2,1},{3,2},{4,7},{5,4},{6,5},{7,6},{8,11},{9,8},{10,9... | collective-permute-start | bytes 589832 | tf_op jit(solution)/shard_map/ppermute | solution.py:30
  53.2 2.5 %collective-permute-start.4 = (bf16[192,512]{1,0:T(8,128)(2,1)S(1)}, bf16[192,512]{1,0:T(8,128)(2,1)S(1)}, u32[]{:S(2)}, u32[]{:S(2)}) collective-permute-start(bf16[192,512]{1,0:T(8,128)(2,1)S(1)} %get-tuple-element.123), channel_id=1, source_target_pairs={{0,1},{1,2},{2,3},{3,0},{4,5},{5,6},{6,7},{7,4},{8,9},{9,10},{10,1... | collective-permute-start | bytes 589832 | tf_op jit(solution)/shard_map/ppermute | solution.py:30
  55.8 3.8 %collective-permute-done.5 = bf16[192,512]{1,0:T(8,128)(2,1)S(1)} collective-permute-done((bf16[192,512]{1,0:T(8,128)(2,1)S(1)}, bf16[192,512]{1,0:T(8,128)(2,1)S(1)}, u32[]{:S(2)}, u32[]{:S(2)}) %collective-permute-start.5) | collective-permute-done | bytes 196640 | tf_op jit(solution)/shard_map/ppermute | solution.py:30
  59.6 2.3 collective-permute-done.4
  62.9 3.5 %all-to-all-start.4 = ((bf16[4,8,24,512]{3,2,1,0:T(8,128)(2,1)}), bf16[4,8,24,512]{3,2,1,0:T(8,128)(2,1)S(1)}, u32[]{:S(2)}, u32[]{:S(2)}) async-start(bf16[4,8,24,512]{3,2,1,0:T(8,128)(2,1)} %broadcast_in_dim.40), calls=%async_computation.4 | async-start | bytes 1572864 | tf_op jit(solution)/shard_map/all_to_all | solution.py:16
  67.2 9.4 %all-to-all-done.4 = bf16[4,8,24,512]{3,2,1,0:T(8,128)(2,1)S(1)} async-done(((bf16[4,8,24,512]{3,2,1,0:T(8,128)(2,1)}), bf16[4,8,24,512]{3,2,1,0:T(8,128)(2,1)S(1)}, u32[]{:S(2)}, u32[]{:S(2)}) %all-to-all-start.4) | async-done | bytes 786464 | tf_op jit(solution)/shard_map/all_to_all | solution.py:16
  76.7 9.7 %all-to-all-start = ((bf16[8,32,512]{2,1,0:T(8,128)(2,1)}), bf16[8,32,512]{2,1,0:T(8,128)(2,1)S(1)}, u32[]{:S(2)}, u32[]{:S(2)}) async-start(bf16[8,32,512]{2,1,0:T(8,128)(2,1)} %pad_maximum_fusion), calls=%async_computation | async-start | bytes 524288 | tf_op jit(solution)/shard_map/all_to_all | solution.py:20
  86.3 1.1 convolution_convert_fusion.1
  87.4 10.8 %all-to-all-done = bf16[8,32,512]{2,1,0:T(8,128)(2,1)S(1)} async-done(((bf16[8,32,512]{2,1,0:T(8,128)(2,1)}), bf16[8,32,512]{2,1,0:T(8,128)(2,1)S(1)}, u32[]{:S(2)}, u32[]{:S(2)}) %all-to-all-start) | async-done | bytes 262176 | tf_op jit(solution)/shard_map/all_to_all | solution.py:20
  98.2 9.1 %all-to-all-start.5 = ((bf16[8,96,256]{2,1,0:T(8,128)(2,1)}), bf16[8,96,256]{2,1,0:T(8,128)(2,1)S(1)}, u32[]{:S(2)}, u32[]{:S(2)}) async-start(bf16[8,96,256]{2,1,0:T(8,128)(2,1)} %bitcast.27), calls=%async_computation.5 | async-start | bytes 786432 | tf_op jit(solution)/shard_map/all_to_all | solution.py:20
  107.4 7.6 %all-to-all-done.5 = bf16[8,96,256]{2,1,0:T(8,128)(2,1)S(1)} async-done(((bf16[8,96,256]{2,1,0:T(8,128)(2,1)}), bf16[8,96,256]{2,1,0:T(8,128)(2,1)S(1)}, u32[]{:S(2)}, u32[]{:S(2)}) %all-to-all-start.5) | async-done | bytes 393248 | tf_op jit(solution)/shard_map/all_to_all | solution.py:20
  115.7 4.8 %all-to-all-start.1 = ((bf16[8,24,512]{2,1,0:T(8,128)(2,1)}), bf16[8,24,512]{2,1,0:T(8,128)(2,1)S(1)}, u32[]{:S(2)}, u32[]{:S(2)}) async-start(bf16[8,24,512]{2,1,0:T(8,128)(2,1)} %broadcast_in_dim.36), calls=%async_computation.1 | async-start | bytes 393216 | tf_op jit(solution)/shard_map/all_to_all | solution.py:16
  121.2 8.2 %collective-permute-start.7 = (f32[96,256]{1,0:T(8,128)S(1)}, f32[96,256]{1,0:T(8,128)S(1)}, u32[]{:S(2)}, u32[]{:S(2)}) collective-permute-start(f32[96,256]{1,0:T(8,128)S(1)} %convert_reduce_fusion), channel_id=1, source_target_pairs={{0,256},{256,0},{1,257},{257,1},{2,258},{258,2},{3,259},{259,3},{4... | collective-permute-start | bytes 294920 | tf_op jit(solution)/shard_map/ppermute | solution.py:71
  129.5 5.9 %collective-permute-done.7 = f32[96,256]{1,0:T(8,128)S(1)} collective-permute-done((f32[96,256]{1,0:T(8,128)S(1)}, f32[96,256]{1,0:T(8,128)S(1)}, u32[]{:S(2)}, u32[]{:S(2)}) %collective-permute-start.7) | collective-permute-done | bytes 98336 | tf_op jit(solution)/shard_map/ppermute | solution.py:71
  135.4 2.2 collective-permute-start.10
  137.6 3.7 %collective-permute-start.9 = (bf16[96,256]{1,0:T(8,128)(2,1)S(1)}, bf16[96,256]{1,0:T(8,128)(2,1)S(1)}, u32[]{:S(2)}, u32[]{:S(2)}) collective-permute-start(bf16[96,256]{1,0:T(8,128)(2,1)S(1)} %add_convert_fusion), channel_id=1, source_target_pairs={{0,128},{64,192},{128,0},{192,64},{1,129},{65,193},{129,1},{193,65... | collective-permute-start | bytes 147464 | tf_op jit(solution)/shard_map/ppermute | solution.py:30
  141.3 2.6 %collective-permute-start.8 = (bf16[96,256]{1,0:T(8,128)(2,1)S(1)}, bf16[96,256]{1,0:T(8,128)(2,1)S(1)}, u32[]{:S(2)}, u32[]{:S(2)}) collective-permute-start(bf16[96,256]{1,0:T(8,128)(2,1)S(1)} %add_convert_fusion), channel_id=1, source_target_pairs={{0,192},{64,0},{128,64},{192,128},{1,193},{65,1},{129,65},{193,129... | collective-permute-start | bytes 147464 | tf_op jit(solution)/shard_map/ppermute | solution.py:30
  144.9 3.5 %all-to-all-start.2 = ((bf16[4,192,512]{2,1,0:T(8,128)(2,1)}), bf16[4,192,512]{2,1,0:T(8,128)(2,1)S(1)}, u32[]{:S(2)}, u32[]{:S(2)}) async-start(bf16[4,192,512]{2,1,0:T(8,128)(2,1)} %broadcast_in_dim.38), calls=%async_computation.2 | async-start | bytes 1572864 | tf_op jit(solution)/shard_map/all_to_all | solution.py:16
  148.5 4.9 %all-gather.1 = bf16[8,96,256]{2,1,0:T(8,128)(2,1)S(1)} all-gather(bf16[4,96,256]{2,1,0:T(8,128)(2,1)S(1)} %pad_maximum_fusion.2), channel_id=3, replica_groups=mesh['zh'=2,'y'=4,'c'=2,'zl'=8,'x'=4] {'c'}, dimensions={0}, use_global_device_ids=true | all-gather | bytes 589824 | tf_op jit(solution)/shard_map/all_gather | solution.py:73
  154.0 3.3 %all-to-all-done.2 = bf16[4,192,512]{2,1,0:T(8,128)(2,1)S(1)} async-done(((bf16[4,192,512]{2,1,0:T(8,128)(2,1)}), bf16[4,192,512]{2,1,0:T(8,128)(2,1)S(1)}, u32[]{:S(2)}, u32[]{:S(2)}) %all-to-all-start.2) | async-done | bytes 786464 | tf_op jit(solution)/shard_map/all_to_all | solution.py:16
  158.4 20.5 %while.10 = (s32[]{:T(128)}, f32[8,4,512]{2,1,0:T(4,128)S(1)}, s32[256]{0:T(256)S(1)}, s32[8]{0:T(128)S(1)}, bf16[2,4,2,2,8,512]{5,4,3,2,1,0:T(8,128)(2,1)S(1)},...) while((s32[]{:T(128)}, f32[8,4,512]{2,1,0:T(4,128)S(1)}, ...), condition=%wide.region_4.5_spmd, body=%wide.region_2.4_spmd.sunk | while | flops 807927808 | bytes 2520225 | solution.py:122
  180.3 21.3 %all_to_all.40 = f32[32,40,128]{2,1,0:T(8,128)S(1)} all-to-all(f32[32,40,128]{2,1,0:T(8,128)S(1)} %bitcast.99), channel_id=1, replica_groups=mesh['zh'=2,'y'=4,'c'=2,'zl'=8,'x'=4] {'y','c','x'}, dimensions={0} | all-to-all | bytes 1310720 | tf_op jit(solution)/shard_map/all_to_all | solution.py:20
  202.9 16.5 %all-to-all-start.7 = ((f32[16,8,128]{2,1,0:T(8,128)}), f32[16,8,128]{2,1,0:T(8,128)S(1)}, u32[]{:S(2)}, u32[]{:S(2)}) async-start(f32[16,8,128]{2,1,0:T(8,128)} %reshape.137), calls=%async_computation.7 | async-start | bytes 131072 | tf_op jit(solution)/shard_map/all_to_all | solution.py:20
  219.5 11.4 %all-to-all-done.7 = f32[16,8,128]{2,1,0:T(8,128)S(1)} async-done(((f32[16,8,128]{2,1,0:T(8,128)}), f32[16,8,128]{2,1,0:T(8,128)S(1)}, u32[]{:S(2)}, u32[]{:S(2)}) %all-to-all-start.7) | async-done | bytes 65568 | tf_op jit(solution)/shard_map/all_to_all | solution.py:20
  (137 shorter events, 33.1 us)
Async XLA Ops:
  0.6 44.7 %copy-start = (bf16[256,512]{1,0:T(8,128)(2,1)S(1)}, bf16[256,512]{1,0:T(8,128)(2,1)}, u32[]{:S(2)}) copy-start(bf16[256,512]{1,0:T(8,128)(2,1)} %param.16) | copy-start | bytes 786436
  2.1 17.6 %collective-permute-start = (bf16[48,256]{1,0:T(8,128)(2,1)S(1)}, bf16[48,256]{1,0:T(8,128)(2,1)S(1)}, u32[]{:S(2)}, u32[]{:S(2)}) collective-permute-start(bf16[48,256]{1,0:T(8,128)(2,1)S(1)} %pad_maximum_fusion.5), channel_id=1, source_target_pairs={{0,256},{256,0},{1,257},{257,1},{2,258},{258,2},{3,259},{259,3},{4... | collective-permute-start | bytes 73736 | tf_op jit(solution)/shard_map/ppermute | solution.py:79
  19.7 20.9 %collective-permute-start.3 = (bf16[96,256]{1,0:T(8,128)(2,1)S(1)}, bf16[96,256]{1,0:T(8,128)(2,1)S(1)}, u32[]{:S(2)}, u32[]{:S(2)}) collective-permute-start(bf16[96,256]{1,0:T(8,128)(2,1)S(1)} %get-tuple-element.129), channel_id=1, source_target_pairs={{0,64},{64,128},{128,192},{192,0},{1,65},{65,129},{129,193},{193,1... | collective-permute-start | bytes 147464 | tf_op jit(solution)/shard_map/ppermute | solution.py:30
  22.9 17.7 %collective-permute-start.2 = (bf16[96,256]{1,0:T(8,128)(2,1)S(1)}, bf16[96,256]{1,0:T(8,128)(2,1)S(1)}, u32[]{:S(2)}, u32[]{:S(2)}) collective-permute-start(bf16[96,256]{1,0:T(8,128)(2,1)S(1)} %get-tuple-element.129), channel_id=1, source_target_pairs={{0,128},{64,192},{128,0},{192,64},{1,129},{65,193},{129,1},{193,65... | collective-permute-start | bytes 147464 | tf_op jit(solution)/shard_map/ppermute | solution.py:30
  27.5 13.2 %collective-permute-start.1 = (bf16[96,256]{1,0:T(8,128)(2,1)S(1)}, bf16[96,256]{1,0:T(8,128)(2,1)S(1)}, u32[]{:S(2)}, u32[]{:S(2)}) collective-permute-start(bf16[96,256]{1,0:T(8,128)(2,1)S(1)} %get-tuple-element.129), channel_id=1, source_target_pairs={{0,192},{64,0},{128,64},{192,128},{1,193},{65,1},{129,65},{193,129... | collective-permute-start | bytes 147464 | tf_op jit(solution)/shard_map/ppermute | solution.py:30
  31.8 30.1 %all-to-all-start.3 = ((bf16[8,24,512]{2,1,0:T(8,128)(2,1)}), bf16[8,24,512]{2,1,0:T(8,128)(2,1)S(1)}, u32[]{:S(2)}, u32[]{:S(2)}) async-start(bf16[8,24,512]{2,1,0:T(8,128)(2,1)} %broadcast_in_dim.39), calls=%async_computation.3 | async-start | bytes 393216 | tf_op jit(solution)/shard_map/all_to_all | solution.py:16
  45.8 10.0 %collective-permute-start.6 = (bf16[192,512]{1,0:T(8,128)(2,1)S(1)}, bf16[192,512]{1,0:T(8,128)(2,1)S(1)}, u32[]{:S(2)}, u32[]{:S(2)}) collective-permute-start(bf16[192,512]{1,0:T(8,128)(2,1)S(1)} %get-tuple-element.124), channel_id=1, source_target_pairs={{0,2},{1,3},{2,0},{3,1},{4,6},{5,7},{6,4},{7,5},{8,10},{9,11},{10,... | collective-permute-start | bytes 589832 | tf_op jit(solution)/shard_map/ppermute | solution.py:30
  50.4 9.1 %collective-permute-start.5 = (bf16[192,512]{1,0:T(8,128)(2,1)S(1)}, bf16[192,512]{1,0:T(8,128)(2,1)S(1)}, u32[]{:S(2)}, u32[]{:S(2)}) collective-permute-start(bf16[192,512]{1,0:T(8,128)(2,1)S(1)} %get-tuple-element.125), channel_id=1, source_target_pairs={{0,3},{1,0},{2,1},{3,2},{4,7},{5,4},{6,5},{7,6},{8,11},{9,8},{10,9... | collective-permute-start | bytes 589832 | tf_op jit(solution)/shard_map/ppermute | solution.py:30
  53.2 8.6 %collective-permute-start.4 = (bf16[192,512]{1,0:T(8,128)(2,1)S(1)}, bf16[192,512]{1,0:T(8,128)(2,1)S(1)}, u32[]{:S(2)}, u32[]{:S(2)}) collective-permute-start(bf16[192,512]{1,0:T(8,128)(2,1)S(1)} %get-tuple-element.123), channel_id=1, source_target_pairs={{0,1},{1,2},{2,3},{3,0},{4,5},{5,6},{6,7},{7,4},{8,9},{9,10},{10,1... | collective-permute-start | bytes 589832 | tf_op jit(solution)/shard_map/ppermute | solution.py:30
  62.9 13.8 %all-to-all-start.4 = ((bf16[4,8,24,512]{3,2,1,0:T(8,128)(2,1)}), bf16[4,8,24,512]{3,2,1,0:T(8,128)(2,1)S(1)}, u32[]{:S(2)}, u32[]{:S(2)}) async-start(bf16[4,8,24,512]{3,2,1,0:T(8,128)(2,1)} %broadcast_in_dim.40), calls=%async_computation.4 | async-start | bytes 1572864 | tf_op jit(solution)/shard_map/all_to_all | solution.py:16
  66.5 19.9 %copy-start.2 = (bf16[512,256]{1,0:T(8,128)(2,1)S(1)}, bf16[512,256]{1,0:T(8,128)(2,1)}, u32[]{:S(2)}) copy-start(bf16[512,256]{1,0:T(8,128)(2,1)} %param.17) | copy-start | bytes 786436
  76.7 21.6 %all-to-all-start = ((bf16[8,32,512]{2,1,0:T(8,128)(2,1)}), bf16[8,32,512]{2,1,0:T(8,128)(2,1)S(1)}, u32[]{:S(2)}, u32[]{:S(2)}) async-start(bf16[8,32,512]{2,1,0:T(8,128)(2,1)} %pad_maximum_fusion), calls=%async_computation | async-start | bytes 524288 | tf_op jit(solution)/shard_map/all_to_all | solution.py:20
  98.2 16.8 %all-to-all-start.5 = ((bf16[8,96,256]{2,1,0:T(8,128)(2,1)}), bf16[8,96,256]{2,1,0:T(8,128)(2,1)S(1)}, u32[]{:S(2)}, u32[]{:S(2)}) async-start(bf16[8,96,256]{2,1,0:T(8,128)(2,1)} %bitcast.27), calls=%async_computation.5 | async-start | bytes 786432 | tf_op jit(solution)/shard_map/all_to_all | solution.py:20
  107.3 22.1 %copy-start.1 = (f32[512,256]{1,0:T(8,128)S(1)}, f32[512,256]{1,0:T(8,128)}, u32[]{:S(2)}) copy-start(f32[512,256]{1,0:T(8,128)} %param.18) | copy-start | bytes 1572868
  115.7 28.2 %all-to-all-start.1 = ((bf16[8,24,512]{2,1,0:T(8,128)(2,1)}), bf16[8,24,512]{2,1,0:T(8,128)(2,1)S(1)}, u32[]{:S(2)}, u32[]{:S(2)}) async-start(bf16[8,24,512]{2,1,0:T(8,128)(2,1)} %broadcast_in_dim.36), calls=%async_computation.1 | async-start | bytes 393216 | tf_op jit(solution)/shard_map/all_to_all | solution.py:16
  121.2 14.2 %collective-permute-start.7 = (f32[96,256]{1,0:T(8,128)S(1)}, f32[96,256]{1,0:T(8,128)S(1)}, u32[]{:S(2)}, u32[]{:S(2)}) collective-permute-start(f32[96,256]{1,0:T(8,128)S(1)} %convert_reduce_fusion), channel_id=1, source_target_pairs={{0,256},{256,0},{1,257},{257,1},{2,258},{258,2},{3,259},{259,3},{4... | collective-permute-start | bytes 294920 | tf_op jit(solution)/shard_map/ppermute | solution.py:71
  135.4 13.1 %collective-permute-start.10 = (bf16[96,256]{1,0:T(8,128)(2,1)S(1)}, bf16[96,256]{1,0:T(8,128)(2,1)S(1)}, u32[]{:S(2)}, u32[]{:S(2)}) collective-permute-start(bf16[96,256]{1,0:T(8,128)(2,1)S(1)} %add_convert_fusion), channel_id=1, source_target_pairs={{0,64},{64,128},{128,192},{192,0},{1,65},{65,129},{129,193},{193,1... | collective-permute-start | bytes 147464 | tf_op jit(solution)/shard_map/ppermute | solution.py:30
  137.6 10.9 %collective-permute-start.9 = (bf16[96,256]{1,0:T(8,128)(2,1)S(1)}, bf16[96,256]{1,0:T(8,128)(2,1)S(1)}, u32[]{:S(2)}, u32[]{:S(2)}) collective-permute-start(bf16[96,256]{1,0:T(8,128)(2,1)S(1)} %add_convert_fusion), channel_id=1, source_target_pairs={{0,128},{64,192},{128,0},{192,64},{1,129},{65,193},{129,1},{193,65... | collective-permute-start | bytes 147464 | tf_op jit(solution)/shard_map/ppermute | solution.py:30
  141.3 7.2 %collective-permute-start.8 = (bf16[96,256]{1,0:T(8,128)(2,1)S(1)}, bf16[96,256]{1,0:T(8,128)(2,1)S(1)}, u32[]{:S(2)}, u32[]{:S(2)}) collective-permute-start(bf16[96,256]{1,0:T(8,128)(2,1)S(1)} %add_convert_fusion), channel_id=1, source_target_pairs={{0,192},{64,0},{128,64},{192,128},{1,193},{65,1},{129,65},{193,129... | collective-permute-start | bytes 147464 | tf_op jit(solution)/shard_map/ppermute | solution.py:30
  144.9 12.4 %all-to-all-start.2 = ((bf16[4,192,512]{2,1,0:T(8,128)(2,1)}), bf16[4,192,512]{2,1,0:T(8,128)(2,1)S(1)}, u32[]{:S(2)}, u32[]{:S(2)}) async-start(bf16[4,192,512]{2,1,0:T(8,128)(2,1)} %broadcast_in_dim.38), calls=%async_computation.2 | async-start | bytes 1572864 | tf_op jit(solution)/shard_map/all_to_all | solution.py:16
  157.7 0.7 copy-start.3
  178.8 0.7 copy-start.4
  202.9 28.1 %all-to-all-start.7 = ((f32[16,8,128]{2,1,0:T(8,128)}), f32[16,8,128]{2,1,0:T(8,128)S(1)}, u32[]{:S(2)}, u32[]{:S(2)}) async-start(f32[16,8,128]{2,1,0:T(8,128)} %reshape.137), calls=%async_computation.7 | async-start | bytes 131072 | tf_op jit(solution)/shard_map/all_to_all | solution.py:20

commit v2 on v1

--- a/solution.py
+++ b/solution.py
@@ -1,6 +1,8 @@
 import jax
 import jax.numpy as jnp
 from jax import lax
+from jax.experimental import pallas as pl
+from jax.experimental.pallas import tpu as pltpu
 from jax.sharding import Mesh, PartitionSpec as P
 
 
@@ -9,6 +11,7 @@
 DOCS = 16
 ROW = ("zh", "y", "c")
 COL = ("zl", "x")
+GROUP = 4
 
 
 def spread(v, axes):
@@ -40,6 +43,100 @@
     return lax.dynamic_slice_in_dim(
         jnp.concatenate([v, v[: n - 1]], axis=0), (n - lax.axis_index(axis)) % n, n, 0
     )
+
+
+def score_kernel(seq_ref, table_ref, gq_ref, gu_ref, aqt_ref, aut_ref, rden_ref, out_ref, p_ref, sum_ref):
+    f32, bf16 = jnp.float32, jnp.bfloat16
+    fj, _ = rden_ref.shape
+    seq = seq_ref[...]
+    gq = gq_ref[...]
+    aqt = aqt_ref[...]
+
+    def precondition(first, slot):
+        for k in range(GROUP):
+            weighted = jnp.where(seq == first + k, aqt, jnp.zeros_like(aqt))
+            outer = jnp.dot(weighted, gq, preferred_element_type=f32)
+            p_ref[slot, k * fj : (k + 1) * fj, :] = (outer * rden_ref[...]).astype(bf16)
+
+    def reduce(first, slot):
+        mapped = lax.dot_general(
+            p_ref[slot], gu_ref[...], (((1,), (1,)), ((), ())), preferred_element_type=f32
+        )
+        for k in range(GROUP):
+            row = jnp.sum(mapped[k * fj : (k + 1) * fj] * aut_ref[...], axis=0, keepdims=True) / D
+            sum_ref[pl.ds(first + k, 1), :] = row
+
+    precondition(0, 0)
+
+    def step(i, carry):
+        first = i * (2 * GROUP)
+        precondition(first + GROUP, 1)
+        reduce(first, 0)
+        precondition(first + 2 * GROUP, 0)
+        reduce(first + GROUP, 1)
+        return carry
+
+    lax.fori_loop(0, S // (2 * GROUP) - 1, step, 0)
+    precondition(S - GROUP, 1)
+    reduce(S - 2 * GROUP, 0)
+    reduce(S - GROUP, 1)
+    docs = jnp.zeros((8, 128), f32)
+    for g in range(S // 8):
+        for x in range(out_ref.shape[0]):
+            docs += jnp.dot(
+                sum_ref[8 * g : 8 * g + 8, 128 * x : 128 * (x + 1)],
+                table_ref[g, x],
+                precision=lax.Precision.HIGHEST,
+                preferred_element_type=f32,
+            )
+    for x in range(out_ref.shape[0]):
+        out_ref[x, :S, :] = sum_ref[:, 128 * x : 128 * (x + 1)].astype(bf16)
+        out_ref[x, S:, :] = docs.astype(bf16)
+
+
+def partial_scores(seq, table, gq, gu, aqt, aut, rden):
+    fj, fi = rden.shape
+    vmem = pl.BlockSpec(memory_space=pltpu.VMEM)
+    return pl.pallas_call(
+        score_kernel,
+        out_shape=jax.ShapeDtypeStruct((table.shape[1], S + 8, 128), jnp.bfloat16),
+        in_specs=[vmem] * 7,
+        out_specs=vmem,
+        scratch_shapes=[
+            pltpu.VMEM((2, GROUP * fj, fi), jnp.bfloat16),
+            pltpu.VMEM((S, gu.shape[0]), jnp.float32),
+        ],
+        compiler_params=pltpu.CompilerParams(vmem_limit_bytes=40 * 1024 * 1024),
+        name="partial_scores",
+    )(seq, table, gq, gu, aqt, aut, rden)
+
+
+def pack_kernel(total_ref, out_ref):
+    total = jnp.concatenate([total_ref[...], jnp.zeros((128 - S - 8, 128), jnp.float32)], axis=0)
+    turned = jnp.transpose(total)
+    lane = lax.broadcasted_iota(jnp.int32, (DOCS, 128), 1)
+    docs = jnp.zeros((DOCS, 128), jnp.float32)
+    for g in range(S // 8):
+        first = S + 8 * g
+        moved = turned[DOCS * g : DOCS * (g + 1)]
+        moved = pltpu.roll(moved, 8 * g, 1) if g else moved
+        docs = jnp.where((lane >= first) & (lane < first + 8), moved, docs)
+    for z in range(8):
+        block = jnp.where(lane < S, turned[16 * z : 16 * z + 16], docs)
+        block = jnp.where(lane[:8] < 2 * S, block[:8], pltpu.roll(block[8:], 2 * S, 1))
+        for h in range(out_ref.shape[0] // 8):
+            out_ref[8 * h + z] = block
+
+
+def pack(total, nz):
+    vmem = pl.BlockSpec(memory_space=pltpu.VMEM)
+    return pl.pallas_call(
+        pack_kernel,
+        out_shape=jax.ShapeDtypeStruct((nz, 8, 128), jnp.float32),
+        in_specs=[vmem],
+        out_specs=vmem,
+        name="pack",
+    )(total)
 
 
 def body(
@@ -95,48 +192,30 @@
     g = spread(g, "zl").reshape(-1, fi)
     g = spread(g, "x")
     g = g.reshape(2, -1, nzh, 2, n, fi)
-    grads = turn(jnp.moveaxis(g, 0, 2), "y")
-    grads = jnp.swapaxes(grads, 0, 1)
-
-    acts = jnp.swapaxes(acts, 0, 1)
+    grads = turn(jnp.moveaxis(g, 1, 0), "y")
+    grads = jnp.transpose(grads, (1, 3, 2, 0, 4, 5))
+
     rot_gq = grads[..., :q, :].reshape(n_query, fi)
     rot_gu = grads[..., q:, :].reshape(n_train, fi)
-    rot_aq = acts[:, :, :q].reshape(n_query, fj)
-    rot_au = acts[:, :, q:].reshape(n_train, fj)
-    denom = eigen_corr + damping
-    act_wide = rot_au.astype(f32)
-    group = 4
-
-    def score_group(first):
-        seq_ids = first + jnp.arange(group, dtype=jnp.int32)
-        member = (query_seq[:, None] == seq_ids[None, :]).astype(bf16)
-        weighted = (member[:, :, None] * rot_gq[:, None, :]).reshape(n_query, group * fi)
-        outer = lax.dot_general(
-            weighted, rot_aq, (((0,), (0,)), ((), ())), preferred_element_type=f32
-        )
-        precond = (outer.reshape(group, fi, fj) / denom[None, :, :]).astype(bf16)
-        mapped = jnp.einsum("ui,sij->usj", rot_gu, precond, preferred_element_type=f32)
-        return jnp.sum(mapped * act_wide[:, None, :], axis=2).T
-
-    starts = jnp.arange(S // group, dtype=jnp.int32) * group
-    partial_scores = lax.map(score_group, starts).reshape(S, n_train) / D
-    doc_table = (train_doc[:, None] == jnp.arange(DOCS, dtype=jnp.int32)[None, :]).astype(f32)
-    counts = jnp.sum(doc_table, axis=0)
-    doc_part = jnp.dot(partial_scores, doc_table, precision=lax.Precision.HIGHEST)
-
-    lanes = nzl * t
-    p = partial_scores.reshape(S, nzl, nx, t)
-    p = jnp.moveaxis(p, 2, 0).reshape(nx, S, lanes)
-    d = jnp.broadcast_to(doc_part.reshape(1, -1, lanes), (nx, S * DOCS // lanes, lanes))
-    p = jnp.concatenate([p, d, jnp.zeros_like(d)], axis=1)
+    rden = (1.0 / (eigen_corr + damping)).T
+    aqt = acts[:, :, :q].reshape(n_query, fj).T
+    aut = acts[:, :, q:].reshape(n_train, fj).astype(f32).T
+    seq = jnp.swapaxes(query_seq.reshape(nzl, nx, q), 0, 1).reshape(1, n_query)
+    doc = jnp.swapaxes(train_doc.reshape(nzl, nx, t), 0, 1).reshape(nx, nzl * t)
+    ids = jnp.arange(DOCS, dtype=jnp.int32)
+    lanes = jnp.arange(128, dtype=jnp.int32)
+    place = jnp.arange(S // 8, dtype=jnp.int32)[:, None, None, None] * DOCS
+    table = (doc[None, :, :, None] + place == lanes).astype(f32)
+    counts = jnp.sum((train_doc[:, None] == ids[None, :]).astype(f32), axis=0)
+    p = partial_scores(seq, table, rot_gq, rot_gu, aqt, aut, rden)
+
     p = jnp.broadcast_to(p[None], (nyc,) + p.shape).reshape((nyc * nx,) + p.shape[1:])
-    p = jnp.sum(exchange(p, ("y", "c", "x")), axis=0)
-    d = p[S : S + S * DOCS // lanes].reshape(S, DOCS)
-    p = jnp.swapaxes(p[:S].reshape(S, nzl, t), 0, 1)
-    p = jnp.concatenate([p, jnp.broadcast_to(d[None], (nzl, S, DOCS))], axis=2)
-    p = jnp.broadcast_to(p[None], (nzh,) + p.shape).reshape(nzh * nzl, -1, 128)
-    p = jnp.sum(exchange(p, ("zh", "zl")), axis=0).reshape(S, t + DOCS)
-    return (p[:, :t], p[:, t:] / counts[None, :])
+    p = exchange(p, ("y", "c", "x"))
+    p = pack(jnp.sum(p.astype(f32), axis=0), nzh * nzl)
+    p = exchange(p, ("zh", "zl"))
+    p = jnp.sum(p, axis=0)
+    p = jnp.concatenate([p[:, : 2 * S], p[:, 2 * S :]], axis=0)
+    return (p[:, :S].T, (p[:, S:] / counts[:, None]).T)
 
 
 def solution(mesh):

time: 234 us -> 215 us (0.919)
  Pallas kernels: 0 us -> 10.5 us
  matrix products: 10.2 us -> 1.48 us
  local copies, waits for them, and re-layouts: 15.6 us -> 7.07 us
  waiting for transfers between devices: 56 us -> 51.9 us
  other arithmetic: 8.45 us -> 5.08 us
  blocking collectives: 30.8 us -> 28.4 us
    pallas_call x0 -> x2, Pallas kernels: none -> 10.5 us  [the longest x1 8.93 us: partial_scores(): pl.pallas_call(score_kernel, out_shape=jax.ShapeDtypeStruct((table.shape[...]
    dot_general x9 -> x0, matrix products: 8.68 us -> none  [the longest x8 8.54 us: score_group(): jnp.einsum('ui,sij->usj', rot_gu, precond, preferred_element_type=f32)]
    add x9 -> x1, other arithmetic: 5.21 us -> 0.07 us  [body(): table = (doc[None, :, :, None] + place == lanes).astype(f32)]
    dynamic_slice x8 -> x0, local copies, waits for them, and re-layouts: 4.71 us -> none  [body(): partial_scores = lax.map(score_group, starts).reshape(S, n_train) / D]
    all_to_all x1, blocking collectives: 21.3 us -> 18.8 us  [exchange(): return lax.all_to_all(parts, axes, 0, 0, tiled=True)]
  transfers between devices with their start and end apart: 18 -> 18, of which waited for: 9 -> 9; matrix products, arithmetic and copies ran while one was open for 2% -> 4% of each run, Pallas kernels for 0% -> 0%
where the time goes in v2:
time: 215 us; the launch traced here: 214 us
  starting transfers between devices  108 us (50%)
  waiting for transfers between devices  51.9 us (24%)
  blocking collectives  28.4 us (13%)
  Pallas kernels  10.5 us (5%)
  local copies, waits for them, and re-layouts  7.07 us (3%)
  other arithmetic  5.08 us (2%)
    all_to_all x3, starting transfers between devices, exchange(): return lax.all_to_all(parts, axes, 0, 0, tiled=True)  35.3 us
    all_to_all x3, waiting for transfers between devices, exchange(): return lax.all_to_all(parts, axes, 0, 0, tiled=True)  29.7 us
    ppermute x9, starting transfers between devices, shift(): return lax.ppermute(v, axis, [(i, (i + k) % n) for i in range(n)])  27.2 us
    all_to_all x4, starting transfers between devices, spread(): lax.all_to_all(jnp.broadcast_to(v[None], (n,) + v.shape), axes, 0, 0, til...  20.7 us
    all_to_all x1, blocking collectives, exchange(): return lax.all_to_all(parts, axes, 0, 0, tiled=True)  18.8 us
    ppermute x1, starting transfers between devices, body(): other = lax.ppermute(g, 'zh', [(0, 1), (1, 0)])  16.2 us
    all_to_all x4, waiting for transfers between devices, spread(): lax.all_to_all(jnp.broadcast_to(v[None], (n,) + v.shape), axes, 0, 0, til...  10.5 us
    pallas_call x1, Pallas kernels, partial_scores(): pl.pallas_call(score_kernel, out_shape=jax.ShapeDtypeStruct((table.shape[...  8.93 us
  transfers between devices with their start and end apart: 18, of which 9 were waited for; matrix products, arithmetic and copies ran while one was open for 4% of the time, Pallas kernels for 0%

profile of v2, /device:TPU:1, one launch (start us, length us, event | category | flops | bytes accessed | tf_op | source)
XLA Modules:
  0.0 213.9 jit_solution(7996213012194207771)
XLA Ops:
  2.1 16.2 %collective-permute-start = (bf16[48,256]{1,0:T(8,128)(2,1)S(1)}, bf16[48,256]{1,0:T(8,128)(2,1)S(1)}, u32[]{:S(2)}, u32[]{:S(2)}) collective-permute-start(bf16[48,256]{1,0:T(8,128)(2,1)S(1)} %pad_maximum_fusion.4), channel_id=1, source_target_pairs={{0,256},{256,0},{1,257},{257,1},{2,258},{258,2},{3,259},{259,3},{4... | collective-permute-start | bytes 73736 | tf_op jit(solution)/shard_map/ppermute | solution.py:176
  18.4 1.3 collective-permute-done
  19.7 4.6 %collective-permute-start.1 = (bf16[96,256]{1,0:T(8,128)(2,1)S(1)}, bf16[96,256]{1,0:T(8,128)(2,1)S(1)}, u32[]{:S(2)}, u32[]{:S(2)}) collective-permute-start(bf16[96,256]{1,0:T(8,128)(2,1)S(1)} %get-tuple-element.8), channel_id=1, source_target_pairs={{0,192},{64,0},{128,64},{192,128},{1,193},{65,1},{129,65},{193,129... | collective-permute-start | bytes 147464 | tf_op jit(solution)/shard_map/ppermute | solution.py:33
  24.4 2.3 %collective-permute-start.2 = (bf16[96,256]{1,0:T(8,128)(2,1)S(1)}, bf16[96,256]{1,0:T(8,128)(2,1)S(1)}, u32[]{:S(2)}, u32[]{:S(2)}) collective-permute-start(bf16[96,256]{1,0:T(8,128)(2,1)S(1)} %get-tuple-element.8), channel_id=1, source_target_pairs={{0,128},{64,192},{128,0},{192,64},{1,129},{65,193},{129,1},{193,65... | collective-permute-start | bytes 147464 | tf_op jit(solution)/shard_map/ppermute | solution.py:33
  26.6 2.6 %collective-permute-start.3 = (bf16[96,256]{1,0:T(8,128)(2,1)S(1)}, bf16[96,256]{1,0:T(8,128)(2,1)S(1)}, u32[]{:S(2)}, u32[]{:S(2)}) collective-permute-start(bf16[96,256]{1,0:T(8,128)(2,1)S(1)} %get-tuple-element.8), channel_id=1, source_target_pairs={{0,64},{64,128},{128,192},{192,0},{1,65},{65,129},{129,193},{193,1... | collective-permute-start | bytes 147464 | tf_op jit(solution)/shard_map/ppermute | solution.py:33
  30.6 8.8 %all-to-all-start.3 = ((bf16[8,24,512]{2,1,0:T(8,128)(2,1)}), bf16[8,24,512]{2,1,0:T(8,128)(2,1)S(1)}, u32[]{:S(2)}, u32[]{:S(2)}) async-start(bf16[8,24,512]{2,1,0:T(8,128)(2,1)} %broadcast_in_dim.15), calls=%async_computation.3 | async-start | bytes 393216 | tf_op jit(solution)/shard_map/all_to_all | solution.py:19
  39.5 4.7 %all-gather = bf16[8,96,256]{2,1,0:T(8,128)(2,1)S(1)} all-gather(bf16[4,96,256]{2,1,0:T(8,128)(2,1)S(1)} %pad_maximum_fusion.1), channel_id=2, replica_groups=mesh['zh'=2,'y'=4,'c'=2,'zl'=8,'x'=4] {'c'}, dimensions={0}, use_global_device_ids=true | all-gather | bytes 589824 | tf_op jit(solution)/shard_map/all_gather | solution.py:180
  44.6 3.1 %collective-permute-start.4 = (bf16[192,512]{1,0:T(8,128)(2,1)S(1)}, bf16[192,512]{1,0:T(8,128)(2,1)S(1)}, u32[]{:S(2)}, u32[]{:S(2)}) collective-permute-start(bf16[192,512]{1,0:T(8,128)(2,1)S(1)} %get-tuple-element.2), channel_id=1, source_target_pairs={{0,1},{1,2},{2,3},{3,0},{4,5},{5,6},{6,7},{7,4},{8,9},{9,10},{10,1... | collective-permute-start | bytes 589832 | tf_op jit(solution)/shard_map/ppermute | solution.py:33
  47.7 3.4 %collective-permute-start.5 = (bf16[192,512]{1,0:T(8,128)(2,1)S(1)}, bf16[192,512]{1,0:T(8,128)(2,1)S(1)}, u32[]{:S(2)}, u32[]{:S(2)}) collective-permute-start(bf16[192,512]{1,0:T(8,128)(2,1)S(1)} %get-tuple-element.4), channel_id=1, source_target_pairs={{0,3},{1,0},{2,1},{3,2},{4,7},{5,4},{6,5},{7,6},{8,11},{9,8},{10,9... | collective-permute-start | bytes 589832 | tf_op jit(solution)/shard_map/ppermute | solution.py:33
  51.1 3.4 %collective-permute-start.6 = (bf16[192,512]{1,0:T(8,128)(2,1)S(1)}, bf16[192,512]{1,0:T(8,128)(2,1)S(1)}, u32[]{:S(2)}, u32[]{:S(2)}) collective-permute-start(bf16[192,512]{1,0:T(8,128)(2,1)S(1)} %get-tuple-element.3), channel_id=1, source_target_pairs={{0,2},{1,3},{2,0},{3,1},{4,6},{5,7},{6,4},{7,5},{8,10},{9,11},{10,... | collective-permute-start | bytes 589832 | tf_op jit(solution)/shard_map/ppermute | solution.py:33
  55.4 4.6 %collective-permute-done.6 = bf16[192,512]{1,0:T(8,128)(2,1)S(1)} collective-permute-done((bf16[192,512]{1,0:T(8,128)(2,1)S(1)}, bf16[192,512]{1,0:T(8,128)(2,1)S(1)}, u32[]{:S(2)}, u32[]{:S(2)}) %collective-permute-start.6) | collective-permute-done | bytes 196640 | tf_op jit(solution)/shard_map/ppermute | solution.py:33
  61.1 3.5 %all-to-all-start.4 = ((bf16[4,8,24,512]{3,2,1,0:T(8,128)(2,1)}), bf16[4,8,24,512]{3,2,1,0:T(8,128)(2,1)S(1)}, u32[]{:S(2)}, u32[]{:S(2)}) async-start(bf16[4,8,24,512]{3,2,1,0:T(8,128)(2,1)} %broadcast_in_dim.16), calls=%async_computation.4 | async-start | bytes 1572864 | tf_op jit(solution)/shard_map/all_to_all | solution.py:19
  65.4 9.4 %all-to-all-done.4 = bf16[4,8,24,512]{3,2,1,0:T(8,128)(2,1)S(1)} async-done(((bf16[4,8,24,512]{3,2,1,0:T(8,128)(2,1)}), bf16[4,8,24,512]{3,2,1,0:T(8,128)(2,1)S(1)}, u32[]{:S(2)}, u32[]{:S(2)}) %all-to-all-start.4) | async-done | bytes 786464 | tf_op jit(solution)/shard_map/all_to_all | solution.py:19
  74.8 9.6 %all-to-all-start = ((bf16[8,32,512]{2,1,0:T(8,128)(2,1)}), bf16[8,32,512]{2,1,0:T(8,128)(2,1)S(1)}, u32[]{:S(2)}, u32[]{:S(2)}) async-start(bf16[8,32,512]{2,1,0:T(8,128)(2,1)} %pad_maximum_fusion), calls=%async_computation | async-start | bytes 524288 | tf_op jit(solution)/shard_map/all_to_all | solution.py:23
  85.7 10.6 %all-to-all-done = bf16[8,32,512]{2,1,0:T(8,128)(2,1)S(1)} async-done(((bf16[8,32,512]{2,1,0:T(8,128)(2,1)}), bf16[8,32,512]{2,1,0:T(8,128)(2,1)S(1)}, u32[]{:S(2)}, u32[]{:S(2)}) %all-to-all-start) | async-done | bytes 262176 | tf_op jit(solution)/shard_map/all_to_all | solution.py:23
  96.3 9.3 %all-to-all-start.5 = ((bf16[8,96,256]{2,1,0:T(8,128)(2,1)}), bf16[8,96,256]{2,1,0:T(8,128)(2,1)S(1)}, u32[]{:S(2)}, u32[]{:S(2)}) async-start(bf16[8,96,256]{2,1,0:T(8,128)(2,1)} %bitcast.21), calls=%async_computation.5 | async-start | bytes 786432 | tf_op jit(solution)/shard_map/all_to_all | solution.py:23
  105.7 7.6 %all-to-all-done.5 = bf16[8,96,256]{2,1,0:T(8,128)(2,1)S(1)} async-done(((bf16[8,96,256]{2,1,0:T(8,128)(2,1)}), bf16[8,96,256]{2,1,0:T(8,128)(2,1)S(1)}, u32[]{:S(2)}, u32[]{:S(2)}) %all-to-all-start.5) | async-done | bytes 393248 | tf_op jit(solution)/shard_map/all_to_all | solution.py:23
  114.0 4.8 %all-to-all-start.1 = ((bf16[8,24,512]{2,1,0:T(8,128)(2,1)}), bf16[8,24,512]{2,1,0:T(8,128)(2,1)S(1)}, u32[]{:S(2)}, u32[]{:S(2)}) async-start(bf16[8,24,512]{2,1,0:T(8,128)(2,1)} %broadcast_in_dim.12), calls=%async_computation.1 | async-start | bytes 393216 | tf_op jit(solution)/shard_map/all_to_all | solution.py:19
  118.9 8.2 %collective-permute-start.7 = (f32[96,256]{1,0:T(8,128)S(1)}, f32[96,256]{1,0:T(8,128)S(1)}, u32[]{:S(2)}, u32[]{:S(2)}) collective-permute-start(f32[96,256]{1,0:T(8,128)S(1)} %convert_reduce_fusion), channel_id=1, source_target_pairs={{0,256},{256,0},{1,257},{257,1},{2,258},{258,2},{3,259},{259,3},{4... | collective-permute-start | bytes 294920 | tf_op jit(solution)/shard_map/ppermute | solution.py:168
  128.3 4.9 %collective-permute-done.7 = f32[96,256]{1,0:T(8,128)S(1)} collective-permute-done((f32[96,256]{1,0:T(8,128)S(1)}, f32[96,256]{1,0:T(8,128)S(1)}, u32[]{:S(2)}, u32[]{:S(2)}) %collective-permute-start.7) | collective-permute-done | bytes 98336 | tf_op jit(solution)/shard_map/ppermute | solution.py:168
  133.2 2.8 %collective-permute-start.8 = (bf16[96,256]{1,0:T(8,128)(2,1)S(1)}, bf16[96,256]{1,0:T(8,128)(2,1)S(1)}, u32[]{:S(2)}, u32[]{:S(2)}) collective-permute-start(bf16[96,256]{1,0:T(8,128)(2,1)S(1)} %add_convert_fusion), channel_id=1, source_target_pairs={{0,192},{64,0},{128,64},{192,128},{1,193},{65,1},{129,65},{193,129... | collective-permute-start | bytes 147464 | tf_op jit(solution)/shard_map/ppermute | solution.py:33
  136.0 3.1 %collective-permute-start.9 = (bf16[96,256]{1,0:T(8,128)(2,1)S(1)}, bf16[96,256]{1,0:T(8,128)(2,1)S(1)}, u32[]{:S(2)}, u32[]{:S(2)}) collective-permute-start(bf16[96,256]{1,0:T(8,128)(2,1)S(1)} %add_convert_fusion), channel_id=1, source_target_pairs={{0,128},{64,192},{128,0},{192,64},{1,129},{65,193},{129,1},{193,65... | collective-permute-start | bytes 147464 | tf_op jit(solution)/shard_map/ppermute | solution.py:33
  139.1 1.9 collective-permute-start.10
  142.0 3.6 %all-to-all-start.2 = ((bf16[4,192,512]{2,1,0:T(8,128)(2,1)}), bf16[4,192,512]{2,1,0:T(8,128)(2,1)S(1)}, u32[]{:S(2)}, u32[]{:S(2)}) async-start(bf16[4,192,512]{2,1,0:T(8,128)(2,1)} %broadcast_in_dim.14), calls=%async_computation.2 | async-start | bytes 1572864 | tf_op jit(solution)/shard_map/all_to_all | solution.py:19
  146.0 5.0 %all-gather.1 = bf16[8,96,256]{2,1,0:T(8,128)(2,1)S(1)} all-gather(bf16[4,96,256]{2,1,0:T(8,128)(2,1)S(1)} %pad_maximum_fusion.2), channel_id=3, replica_groups=mesh['zh'=2,'y'=4,'c'=2,'zl'=8,'x'=4] {'c'}, dimensions={0}, use_global_device_ids=true | all-gather | bytes 589824 | tf_op jit(solution)/shard_map/all_gather | solution.py:170
  152.1 1.2 copy.42
  153.5 1.1 all-to-all-done.2
  155.1 8.9 %partial_scores.1 = bf16[4,40,128]{2,1,0:T(8,128)(2,1)S(1)} custom-call(s32[1,256]{1,0:T(1,128)S(1)} %reshape.85.seq_ref, f32[4,4,128,128]{3,2,1,0:T(8,128)S(1)} %fusion.table_ref, bf16[256,512]{1,0:T(8,128)(2,1)S(1)} %bitcast.56, bf16[512,512]{1,0:T(8,128)(2,1)S(1)} %bitcast.55, bf16[256,256]{1,0:T(8,128)(2,1)S(1)} %bitcast.57, f32[256,512]{1,0:T(8,128)S(1)} %bitcast.54, ...), custom_call_target="tpu_custom_call" | custom-call | tf_op jit(solution)/shard_map/partial_scores/pallas_call | solution.py:100
  164.1 18.8 %all_to_all.40 = bf16[32,40,128]{2,1,0:T(8,128)(2,1)S(1)} all-to-all(bf16[32,40,128]{2,1,0:T(8,128)(2,1)S(1)} %bitcast.70), channel_id=1, replica_groups=mesh['zh'=2,'y'=4,'c'=2,'zl'=8,'x'=4] {'y','c','x'}, dimensions={0} | all-to-all | bytes 655360 | tf_op jit(solution)/shard_map/all_to_all | solution.py:23
  183.5 1.6 pack.1
  185.1 16.4 %all-to-all-start.7 = ((f32[16,8,128]{2,1,0:T(8,128)}), f32[16,8,128]{2,1,0:T(8,128)S(1)}, u32[]{:S(2)}, u32[]{:S(2)}) async-start(f32[16,8,128]{2,1,0:T(8,128)} %pack.1), calls=%async_computation.7 | async-start | bytes 131072 | tf_op jit(solution)/shard_map/all_to_all | solution.py:23
  201.6 11.5 %all-to-all-done.7 = f32[16,8,128]{2,1,0:T(8,128)S(1)} async-done(((f32[16,8,128]{2,1,0:T(8,128)}), f32[16,8,128]{2,1,0:T(8,128)S(1)}, u32[]{:S(2)}, u32[]{:S(2)}) %all-to-all-start.7) | async-done | bytes 65568 | tf_op jit(solution)/shard_map/all_to_all | solution.py:23
  (75 shorter events, 13.3 us)
Async XLA Ops:
  0.6 43.5 %copy-start = (bf16[256,512]{1,0:T(8,128)(2,1)S(1)}, bf16[256,512]{1,0:T(8,128)(2,1)}, u32[]{:S(2)}) copy-start(bf16[256,512]{1,0:T(8,128)(2,1)} %param.14) | copy-start | bytes 786436
  2.1 17.6 %collective-permute-start = (bf16[48,256]{1,0:T(8,128)(2,1)S(1)}, bf16[48,256]{1,0:T(8,128)(2,1)S(1)}, u32[]{:S(2)}, u32[]{:S(2)}) collective-permute-start(bf16[48,256]{1,0:T(8,128)(2,1)S(1)} %pad_maximum_fusion.4), channel_id=1, source_target_pairs={{0,256},{256,0},{1,257},{257,1},{2,258},{258,2},{3,259},{259,3},{4... | collective-permute-start | bytes 73736 | tf_op jit(solution)/shard_map/ppermute | solution.py:176
  19.7 19.7 %collective-permute-start.1 = (bf16[96,256]{1,0:T(8,128)(2,1)S(1)}, bf16[96,256]{1,0:T(8,128)(2,1)S(1)}, u32[]{:S(2)}, u32[]{:S(2)}) collective-permute-start(bf16[96,256]{1,0:T(8,128)(2,1)S(1)} %get-tuple-element.8), channel_id=1, source_target_pairs={{0,192},{64,0},{128,64},{192,128},{1,193},{65,1},{129,65},{193,129... | collective-permute-start | bytes 147464 | tf_op jit(solution)/shard_map/ppermute | solution.py:33
  24.4 15.1 %collective-permute-start.2 = (bf16[96,256]{1,0:T(8,128)(2,1)S(1)}, bf16[96,256]{1,0:T(8,128)(2,1)S(1)}, u32[]{:S(2)}, u32[]{:S(2)}) collective-permute-start(bf16[96,256]{1,0:T(8,128)(2,1)S(1)} %get-tuple-element.8), channel_id=1, source_target_pairs={{0,128},{64,192},{128,0},{192,64},{1,129},{65,193},{129,1},{193,65... | collective-permute-start | bytes 147464 | tf_op jit(solution)/shard_map/ppermute | solution.py:33
  26.6 12.8 %collective-permute-start.3 = (bf16[96,256]{1,0:T(8,128)(2,1)S(1)}, bf16[96,256]{1,0:T(8,128)(2,1)S(1)}, u32[]{:S(2)}, u32[]{:S(2)}) collective-permute-start(bf16[96,256]{1,0:T(8,128)(2,1)S(1)} %get-tuple-element.8), channel_id=1, source_target_pairs={{0,64},{64,128},{128,192},{192,0},{1,65},{65,129},{129,193},{193,1... | collective-permute-start | bytes 147464 | tf_op jit(solution)/shard_map/ppermute | solution.py:33
  30.6 29.5 %all-to-all-start.3 = ((bf16[8,24,512]{2,1,0:T(8,128)(2,1)}), bf16[8,24,512]{2,1,0:T(8,128)(2,1)S(1)}, u32[]{:S(2)}, u32[]{:S(2)}) async-start(bf16[8,24,512]{2,1,0:T(8,128)(2,1)} %broadcast_in_dim.15), calls=%async_computation.3 | async-start | bytes 393216 | tf_op jit(solution)/shard_map/all_to_all | solution.py:19
  44.6 10.0 %collective-permute-start.4 = (bf16[192,512]{1,0:T(8,128)(2,1)S(1)}, bf16[192,512]{1,0:T(8,128)(2,1)S(1)}, u32[]{:S(2)}, u32[]{:S(2)}) collective-permute-start(bf16[192,512]{1,0:T(8,128)(2,1)S(1)} %get-tuple-element.2), channel_id=1, source_target_pairs={{0,1},{1,2},{2,3},{3,0},{4,5},{5,6},{6,7},{7,4},{8,9},{9,10},{10,1... | collective-permute-start | bytes 589832 | tf_op jit(solution)/shard_map/ppermute | solution.py:33
  47.7 7.7 %collective-permute-start.5 = (bf16[192,512]{1,0:T(8,128)(2,1)S(1)}, bf16[192,512]{1,0:T(8,128)(2,1)S(1)}, u32[]{:S(2)}, u32[]{:S(2)}) collective-permute-start(bf16[192,512]{1,0:T(8,128)(2,1)S(1)} %get-tuple-element.4), channel_id=1, source_target_pairs={{0,3},{1,0},{2,1},{3,2},{4,7},{5,4},{6,5},{7,6},{8,11},{9,8},{10,9... | collective-permute-start | bytes 589832 | tf_op jit(solution)/shard_map/ppermute | solution.py:33
  51.1 8.9 %collective-permute-start.6 = (bf16[192,512]{1,0:T(8,128)(2,1)S(1)}, bf16[192,512]{1,0:T(8,128)(2,1)S(1)}, u32[]{:S(2)}, u32[]{:S(2)}) collective-permute-start(bf16[192,512]{1,0:T(8,128)(2,1)S(1)} %get-tuple-element.3), channel_id=1, source_target_pairs={{0,2},{1,3},{2,0},{3,1},{4,6},{5,7},{6,4},{7,5},{8,10},{9,11},{10,... | collective-permute-start | bytes 589832 | tf_op jit(solution)/shard_map/ppermute | solution.py:33
  61.1 13.7 %all-to-all-start.4 = ((bf16[4,8,24,512]{3,2,1,0:T(8,128)(2,1)}), bf16[4,8,24,512]{3,2,1,0:T(8,128)(2,1)S(1)}, u32[]{:S(2)}, u32[]{:S(2)}) async-start(bf16[4,8,24,512]{3,2,1,0:T(8,128)(2,1)} %broadcast_in_dim.16), calls=%async_computation.4 | async-start | bytes 1572864 | tf_op jit(solution)/shard_map/all_to_all | solution.py:19
  64.6 19.8 %copy-start.3 = (s32[512]{0:T(512)S(1)}, s32[512]{0:T(512)}, u32[]{:S(2)}) copy-start(s32[512]{0:T(512)} %param.19) | copy-start | bytes 6148
  64.6 20.0 %copy-start.2 = (bf16[512,256]{1,0:T(8,128)(2,1)S(1)}, bf16[512,256]{1,0:T(8,128)(2,1)}, u32[]{:S(2)}) copy-start(bf16[512,256]{1,0:T(8,128)(2,1)} %param.15) | copy-start | bytes 786436
  74.8 21.5 %all-to-all-start = ((bf16[8,32,512]{2,1,0:T(8,128)(2,1)}), bf16[8,32,512]{2,1,0:T(8,128)(2,1)S(1)}, u32[]{:S(2)}, u32[]{:S(2)}) async-start(bf16[8,32,512]{2,1,0:T(8,128)(2,1)} %pad_maximum_fusion), calls=%async_computation | async-start | bytes 524288 | tf_op jit(solution)/shard_map/all_to_all | solution.py:23
  96.3 17.0 %all-to-all-start.5 = ((bf16[8,96,256]{2,1,0:T(8,128)(2,1)}), bf16[8,96,256]{2,1,0:T(8,128)(2,1)S(1)}, u32[]{:S(2)}, u32[]{:S(2)}) async-start(bf16[8,96,256]{2,1,0:T(8,128)(2,1)} %bitcast.21), calls=%async_computation.5 | async-start | bytes 786432 | tf_op jit(solution)/shard_map/all_to_all | solution.py:23
  105.7 21.8 %copy-start.1 = (f32[512,256]{1,0:T(8,128)S(1)}, f32[512,256]{1,0:T(8,128)}, u32[]{:S(2)}) copy-start(f32[512,256]{1,0:T(8,128)} %param.16) | copy-start | bytes 1572868
  114.0 27.0 %all-to-all-start.1 = ((bf16[8,24,512]{2,1,0:T(8,128)(2,1)}), bf16[8,24,512]{2,1,0:T(8,128)(2,1)S(1)}, u32[]{:S(2)}, u32[]{:S(2)}) async-start(bf16[8,24,512]{2,1,0:T(8,128)(2,1)} %broadcast_in_dim.12), calls=%async_computation.1 | async-start | bytes 393216 | tf_op jit(solution)/shard_map/all_to_all | solution.py:19
  118.9 14.3 %collective-permute-start.7 = (f32[96,256]{1,0:T(8,128)S(1)}, f32[96,256]{1,0:T(8,128)S(1)}, u32[]{:S(2)}, u32[]{:S(2)}) collective-permute-start(f32[96,256]{1,0:T(8,128)S(1)} %convert_reduce_fusion), channel_id=1, source_target_pairs={{0,256},{256,0},{1,257},{257,1},{2,258},{258,2},{3,259},{259,3},{4... | collective-permute-start | bytes 294920 | tf_op jit(solution)/shard_map/ppermute | solution.py:168
  133.2 12.8 %collective-permute-start.8 = (bf16[96,256]{1,0:T(8,128)(2,1)S(1)}, bf16[96,256]{1,0:T(8,128)(2,1)S(1)}, u32[]{:S(2)}, u32[]{:S(2)}) collective-permute-start(bf16[96,256]{1,0:T(8,128)(2,1)S(1)} %add_convert_fusion), channel_id=1, source_target_pairs={{0,192},{64,0},{128,64},{192,128},{1,193},{65,1},{129,65},{193,129... | collective-permute-start | bytes 147464 | tf_op jit(solution)/shard_map/ppermute | solution.py:33
  136.0 10.0 %collective-permute-start.9 = (bf16[96,256]{1,0:T(8,128)(2,1)S(1)}, bf16[96,256]{1,0:T(8,128)(2,1)S(1)}, u32[]{:S(2)}, u32[]{:S(2)}) collective-permute-start(bf16[96,256]{1,0:T(8,128)(2,1)S(1)} %add_convert_fusion), channel_id=1, source_target_pairs={{0,128},{64,192},{128,0},{192,64},{1,129},{65,193},{129,1},{193,65... | collective-permute-start | bytes 147464 | tf_op jit(solution)/shard_map/ppermute | solution.py:33
  139.1 6.9 %collective-permute-start.10 = (bf16[96,256]{1,0:T(8,128)(2,1)S(1)}, bf16[96,256]{1,0:T(8,128)(2,1)S(1)}, u32[]{:S(2)}, u32[]{:S(2)}) collective-permute-start(bf16[96,256]{1,0:T(8,128)(2,1)S(1)} %add_convert_fusion), channel_id=1, source_target_pairs={{0,64},{64,128},{128,192},{192,0},{1,65},{65,129},{129,193},{193,1... | collective-permute-start | bytes 147464 | tf_op jit(solution)/shard_map/ppermute | solution.py:33
  142.0 3.8 %copy-start.4 = (s32[256]{0:T(256)S(1)}, s32[256]{0:T(256)}, u32[]{:S(2)}) copy-start(s32[256]{0:T(256)} %param.18) | copy-start | bytes 3076
  142.0 12.7 %all-to-all-start.2 = ((bf16[4,192,512]{2,1,0:T(8,128)(2,1)}), bf16[4,192,512]{2,1,0:T(8,128)(2,1)S(1)}, u32[]{:S(2)}, u32[]{:S(2)}) async-start(bf16[4,192,512]{2,1,0:T(8,128)(2,1)} %broadcast_in_dim.14), calls=%async_computation.2 | async-start | bytes 1572864 | tf_op jit(solution)/shard_map/all_to_all | solution.py:19
  185.1 28.0 %all-to-all-start.7 = ((f32[16,8,128]{2,1,0:T(8,128)}), f32[16,8,128]{2,1,0:T(8,128)S(1)}, u32[]{:S(2)}, u32[]{:S(2)}) async-start(f32[16,8,128]{2,1,0:T(8,128)} %pack.1), calls=%async_computation.7 | async-start | bytes 131072 | tf_op jit(solution)/shard_map/all_to_all | solution.py:23

commit v3 on v2

--- a/solution.py
+++ b/solution.py
@@ -11,7 +11,7 @@
 DOCS = 16
 ROW = ("zh", "y", "c")
 COL = ("zl", "x")
-GROUP = 4
+GROUP = 8
 
 
 def spread(v, axes):
@@ -33,16 +33,9 @@
     return lax.ppermute(v, axis, [(i, (i + k) % n) for i in range(n)])
 
 
-def around(v, axis):
-    n = lax.axis_size(axis)
-    return jnp.stack([v] + [shift(v, axis, n - k) for k in range(1, n)])
-
-
-def turn(v, axis):
-    n = lax.axis_size(axis)
-    return lax.dynamic_slice_in_dim(
-        jnp.concatenate([v, v[: n - 1]], axis=0), (n - lax.axis_index(axis)) % n, n, 0
-    )
+def meet(v, axis, partner, first):
+    other = lax.ppermute(v, axis, list(enumerate(partner)))
+    return jnp.concatenate([jnp.where(first, v, other), jnp.where(first, other, v)], axis=0)
 
 
 def score_kernel(seq_ref, table_ref, gq_ref, gu_ref, aqt_ref, aut_ref, rden_ref, out_ref, p_ref, sum_ref):
@@ -54,7 +47,7 @@
 
     def precondition(first, slot):
         for k in range(GROUP):
-            weighted = jnp.where(seq == first + k, aqt, jnp.zeros_like(aqt))
+            weighted = jnp.where(seq == jnp.asarray(first + k).astype(f32), aqt, jnp.zeros_like(aqt))
             outer = jnp.dot(weighted, gq, preferred_element_type=f32)
             p_ref[slot, k * fj : (k + 1) * fj, :] = (outer * rden_ref[...]).astype(bf16)
 
@@ -82,24 +75,32 @@
     reduce(S - GROUP, 1)
     docs = jnp.zeros((8, 128), f32)
     for g in range(S // 8):
-        for x in range(out_ref.shape[0]):
+        for m in range(sum_ref.shape[1] // 128):
             docs += jnp.dot(
-                sum_ref[8 * g : 8 * g + 8, 128 * x : 128 * (x + 1)],
-                table_ref[g, x],
+                sum_ref[8 * g : 8 * g + 8, 128 * m : 128 * (m + 1)],
+                table_ref[g, m],
                 precision=lax.Precision.HIGHEST,
                 preferred_element_type=f32,
             )
-    for x in range(out_ref.shape[0]):
-        out_ref[x, :S, :] = sum_ref[:, 128 * x : 128 * (x + 1)].astype(bf16)
-        out_ref[x, S:, :] = docs.astype(bf16)
-
-
-def partial_scores(seq, table, gq, gu, aqt, aut, rden):
+    half = S // 2
+    low = lax.broadcasted_iota(jnp.int32, (half, 128), 1) < 64
+    for m in range(sum_ref.shape[1] // 128):
+        a = sum_ref[:half, 128 * m : 128 * (m + 1)]
+        b = sum_ref[half:, 128 * m : 128 * (m + 1)]
+        even = jnp.where(low, a, pltpu.roll(b, 64, 1)).astype(bf16)
+        odd = jnp.where(low, pltpu.roll(a, 64, 1), b).astype(bf16)
+        for z, rows in ((2 * m, even), (2 * m + 1, odd)):
+            for h in range(out_ref.shape[0] // 8):
+                out_ref[8 * h + z, :half, :] = rows
+                out_ref[8 * h + z, half:, :] = docs.astype(bf16)
+
+
+def partial_scores(seq, table, gq, gu, aqt, aut, rden, nz):
     fj, fi = rden.shape
     vmem = pl.BlockSpec(memory_space=pltpu.VMEM)
     return pl.pallas_call(
         score_kernel,
-        out_shape=jax.ShapeDtypeStruct((table.shape[1], S + 8, 128), jnp.bfloat16),
+        out_shape=jax.ShapeDtypeStruct((nz, S // 2 + 8, 128), jnp.bfloat16),
         in_specs=[vmem] * 7,
         out_specs=vmem,
         scratch_shapes=[
@@ -112,27 +113,29 @@
 
 
 def pack_kernel(total_ref, out_ref):
-    total = jnp.concatenate([total_ref[...], jnp.zeros((128 - S - 8, 128), jnp.float32)], axis=0)
+    half = S // 2
+    rows = total_ref.shape[0]
+    total = jnp.concatenate([total_ref[...], jnp.zeros((128 - rows, 128), jnp.float32)], axis=0)
     turned = jnp.transpose(total)
     lane = lax.broadcasted_iota(jnp.int32, (DOCS, 128), 1)
     docs = jnp.zeros((DOCS, 128), jnp.float32)
     for g in range(S // 8):
         first = S + 8 * g
-        moved = turned[DOCS * g : DOCS * (g + 1)]
-        moved = pltpu.roll(moved, 8 * g, 1) if g else moved
+        moved = pltpu.roll(turned[DOCS * g : DOCS * (g + 1)], half + 8 * g, 1)
         docs = jnp.where((lane >= first) & (lane < first + 8), moved, docs)
-    for z in range(8):
-        block = jnp.where(lane < S, turned[16 * z : 16 * z + 16], docs)
+    for x in range(4):
+        block = jnp.where(lane < S, pltpu.roll(turned[64 + 16 * x : 80 + 16 * x], half, 1), docs)
+        block = jnp.where(lane < half, turned[16 * x : 16 * x + 16], block)
         block = jnp.where(lane[:8] < 2 * S, block[:8], pltpu.roll(block[8:], 2 * S, 1))
-        for h in range(out_ref.shape[0] // 8):
-            out_ref[8 * h + z] = block
-
-
-def pack(total, nz):
+        for h in range(out_ref.shape[0] // 4):
+            out_ref[4 * h + x] = block
+
+
+def pack(total, n):
     vmem = pl.BlockSpec(memory_space=pltpu.VMEM)
     return pl.pallas_call(
         pack_kernel,
-        out_shape=jax.ShapeDtypeStruct((nz, 8, 128), jnp.float32),
+        out_shape=jax.ShapeDtypeStruct((n, 8, 128), jnp.float32),
         in_specs=[vmem],
         out_specs=vmem,
         name="pack",
@@ -162,13 +165,15 @@
     a = spread(jnp.concatenate([query_acts, train_acts], axis=0), "zl")
     a = spread(a, "x")
     act_part = jnp.dot(a.reshape(-1, a.shape[-1]), act_basis, preferred_element_type=f32)
-    act_part = act_part.astype(bf16).reshape(nyc, -1, fj)
+    act_part = act_part.reshape(nyc, -1, fj)
     a = exchange(act_part, ("y", "c"))
     a = jnp.sum(a.astype(f32), axis=0)
     a = (a + lax.ppermute(a, "zh", [(0, 1), (1, 0)])).astype(bf16)
-    a = around(a, "y")
+    y = lax.axis_index("y")
+    a = meet(a[None], "y", (1, 0, 3, 2), y % 2 == 0)
+    a = meet(a, "y", (3, 2, 1, 0), y < 2)
     a = lax.all_gather(a, "c")
-    acts = turn(jnp.swapaxes(a, 0, 1), "y").reshape(nx, nzl, n, fj)
+    acts = jnp.swapaxes(a, 0, 1).reshape(nx, nzl, n, fj)
 
     g = jnp.concatenate(
         [query_grads[:q], train_grads[:t], query_grads[q:], train_grads[t:]], axis=0
@@ -176,7 +181,9 @@
     other = lax.ppermute(g, "zh", [(0, 1), (1, 0)])
     first = lax.axis_index("zh") == 0
     g = jnp.concatenate([jnp.where(first, g, other), jnp.where(first, other, g)], axis=0)
-    g = around(g, "y")
+    g = g.reshape(nzh, -1, fj)
+    g = meet(g, "y", (1, 0, 3, 2), y % 2 == 0)
+    g = meet(g, "y", (3, 2, 1, 0), y < 2)
     g = lax.all_gather(g, "c")
     g = g.reshape(n_query + n_train, -1)
     grad_part = jnp.dot(g, grad_basis, preferred_element_type=f32)
@@ -192,27 +199,26 @@
     g = spread(g, "zl").reshape(-1, fi)
     g = spread(g, "x")
     g = g.reshape(2, -1, nzh, 2, n, fi)
-    grads = turn(jnp.moveaxis(g, 1, 0), "y")
-    grads = jnp.transpose(grads, (1, 3, 2, 0, 4, 5))
+    grads = jnp.transpose(g, (2, 1, 0, 3, 4, 5))
 
     rot_gq = grads[..., :q, :].reshape(n_query, fi)
     rot_gu = grads[..., q:, :].reshape(n_train, fi)
     rden = (1.0 / (eigen_corr + damping)).T
+    acts = jnp.swapaxes(acts, 0, 1)
     aqt = acts[:, :, :q].reshape(n_query, fj).T
     aut = acts[:, :, q:].reshape(n_train, fj).astype(f32).T
-    seq = jnp.swapaxes(query_seq.reshape(nzl, nx, q), 0, 1).reshape(1, n_query)
-    doc = jnp.swapaxes(train_doc.reshape(nzl, nx, t), 0, 1).reshape(nx, nzl * t)
+    seq = query_seq.astype(f32).reshape(1, n_query)
+    doc = train_doc.reshape(-1, 128)
     ids = jnp.arange(DOCS, dtype=jnp.int32)
     lanes = jnp.arange(128, dtype=jnp.int32)
     place = jnp.arange(S // 8, dtype=jnp.int32)[:, None, None, None] * DOCS
     table = (doc[None, :, :, None] + place == lanes).astype(f32)
     counts = jnp.sum((train_doc[:, None] == ids[None, :]).astype(f32), axis=0)
-    p = partial_scores(seq, table, rot_gq, rot_gu, aqt, aut, rden)
-
-    p = jnp.broadcast_to(p[None], (nyc,) + p.shape).reshape((nyc * nx,) + p.shape[1:])
+    p = partial_scores(seq, table, rot_gq, rot_gu, aqt, aut, rden, nzh * nzl)
+
+    p = exchange(p, ("zh", "zl"))
+    p = pack(jnp.sum(p.astype(f32), axis=0), nyc * nx)
     p = exchange(p, ("y", "c", "x"))
-    p = pack(jnp.sum(p.astype(f32), axis=0), nzh * nzl)
-    p = exchange(p, ("zh", "zl"))
     p = jnp.sum(p, axis=0)
     p = jnp.concatenate([p[:, : 2 * S], p[:, 2 * S :]], axis=0)
     return (p[:, :S].T, (p[:, S:] / counts[:, None]).T)

time: 215 us -> 215 us (level)
  starting transfers between devices: 108 us -> 95.7 us
  waiting for transfers between devices: 51.9 us -> 64 us
    ppermute x9 -> x3, starting transfers between devices: 27.2 us -> 9.94 us  [shift(): return lax.ppermute(v, axis, [(i, (i + k) % n) for i in range(n)])]
    ppermute x0 -> x4, starting transfers between devices: none -> 12.8 us  [meet(): other = lax.ppermute(v, axis, list(enumerate(partner)))]
    all_to_all x4, waiting for transfers between devices: 10.5 us -> 22.8 us  [spread(): lax.all_to_all(jnp.broadcast_to(v[None], (n,) + v.shape), axes, 0, 0, til...]
    all_to_all x3, starting transfers between devices: 35.3 us -> 27.8 us  [exchange(): return lax.all_to_all(parts, axes, 0, 0, tiled=True)]
    ppermute x1, waiting for transfers between devices: 4.85 us -> 0.99 us  [body(): a = (a + lax.ppermute(a, 'zh', [(0, 1), (1, 0)])).astype(bf16)]
    ppermute x0 -> x4, waiting for transfers between devices: none -> 3.31 us  [meet(): other = lax.ppermute(v, axis, list(enumerate(partner)))]
    all_gather x1, blocking collectives: 5.02 us -> 2.85 us  [body(): a = lax.all_gather(a, 'c')]
    ppermute x9 -> x3, waiting for transfers between devices: 5.47 us -> 5.44 us  [shift(): return lax.ppermute(v, axis, [(i, (i + k) % n) for i in range(n)])]
  transfers between devices with their start and end apart: 18 -> 16, of which waited for: 9 -> 12; matrix products, arithmetic and copies ran while one was open for 4% -> 4% of each run, Pallas kernels for 0% -> 0%
where the time goes in v3:
time: 215 us; the launch traced here: 213 us
  starting transfers between devices  95.7 us (45%)
  waiting for transfers between devices  64 us (30%)
  blocking collectives  28.6 us (13%)
  Pallas kernels  10.4 us (5%)
  local copies, waits for them, and re-layouts  7.46 us (3%)
  other arithmetic  3.9 us (2%)
    all_to_all x3, waiting for transfers between devices, exchange(): return lax.all_to_all(parts, axes, 0, 0, tiled=True)  30.2 us
    all_to_all x3, starting transfers between devices, exchange(): return lax.all_to_all(parts, axes, 0, 0, tiled=True)  27.8 us
    all_to_all x4, waiting for transfers between devices, spread(): lax.all_to_all(jnp.broadcast_to(v[None], (n,) + v.shape), axes, 0, 0, til...  22.8 us
    all_to_all x4, starting transfers between devices, spread(): lax.all_to_all(jnp.broadcast_to(v[None], (n,) + v.shape), axes, 0, 0, til...  20.6 us
    all_to_all x1, blocking collectives, exchange(): return lax.all_to_all(parts, axes, 0, 0, tiled=True)  20.5 us
    ppermute x1, starting transfers between devices, body(): other = lax.ppermute(g, 'zh', [(0, 1), (1, 0)])  16.2 us
    ppermute x4, starting transfers between devices, meet(): other = lax.ppermute(v, axis, list(enumerate(partner)))  12.8 us
    ppermute x3, starting transfers between devices, shift(): return lax.ppermute(v, axis, [(i, (i + k) % n) for i in range(n)])  9.94 us
  transfers between devices with their start and end apart: 16, of which 12 were waited for; matrix products, arithmetic and copies ran while one was open for 4% of the time, Pallas kernels for 0%

profile of v3, /device:TPU:1, one launch (start us, length us, event | category | flops | bytes accessed | tf_op | source)
XLA Modules:
  0.0 213.4 jit_solution(2200858614182787914)
XLA Ops:
  2.1 16.2 %collective-permute-start = (bf16[48,256]{1,0:T(8,128)(2,1)S(1)}, bf16[48,256]{1,0:T(8,128)(2,1)S(1)}, u32[]{:S(2)}, u32[]{:S(2)}) collective-permute-start(bf16[48,256]{1,0:T(8,128)(2,1)S(1)} %pad_maximum_fusion.6), channel_id=1, source_target_pairs={{0,256},{256,0},{1,257},{257,1},{2,258},{258,2},{3,259},{259,3},{4... | collective-permute-start | bytes 73736 | tf_op jit(solution)/shard_map/ppermute | solution.py:181
  18.4 1.3 collective-permute-done
  19.7 3.2 %collective-permute-start.1 = (bf16[2,48,256]{2,1,0:T(8,128)(2,1)S(1)}, bf16[2,48,256]{2,1,0:T(8,128)(2,1)S(1)}, u32[]{:S(2)}, u32[]{:S(2)}) collective-permute-start(bf16[2,48,256]{2,1,0:T(8,128)(2,1)S(1)} %bitcast.65), channel_id=1, source_target_pairs={{0,64},{64,0},{128,192},{192,128},{1,65},{65,1},{129,193},{193,129... | collective-permute-start | bytes 147464 | tf_op jit(solution)/shard_map/ppermute | solution.py:37
  22.9 1.6 collective-permute-done.1
  24.6 4.6 %collective-permute-start.2 = (bf16[4,48,256]{2,1,0:T(8,128)(2,1)S(1)}, bf16[4,48,256]{2,1,0:T(8,128)(2,1)S(1)}, u32[]{:S(2)}, u32[]{:S(2)}) collective-permute-start(bf16[4,48,256]{2,1,0:T(8,128)(2,1)S(1)} %pad_maximum_fusion.3), channel_id=1, source_target_pairs={{0,192},{64,128},{128,64},{192,0},{1,193},{65,129},{129,65},{193,1... | collective-permute-start | bytes 294920 | tf_op jit(solution)/shard_map/ppermute | solution.py:37
  30.6 8.8 %all-to-all-start.3 = ((bf16[8,24,512]{2,1,0:T(8,128)(2,1)}), bf16[8,24,512]{2,1,0:T(8,128)(2,1)S(1)}, u32[]{:S(2)}, u32[]{:S(2)}) async-start(bf16[8,24,512]{2,1,0:T(8,128)(2,1)} %broadcast_in_dim.15), calls=%async_computation.3 | async-start | bytes 393216 | tf_op jit(solution)/shard_map/all_to_all | solution.py:19
  39.5 5.2 %all-gather = bf16[16,48,256]{2,1,0:T(8,128)(2,1)S(1)} all-gather(bf16[8,48,256]{2,1,0:T(8,128)(2,1)S(1)} %pad_maximum_fusion.1), channel_id=2, replica_groups=mesh['zh'=2,'y'=4,'c'=2,'zl'=8,'x'=4] {'c'}, dimensions={0}, use_global_device_ids=true | all-gather | bytes 589824 | tf_op jit(solution)/shard_map/all_gather | solution.py:187
  45.2 3.1 %collective-permute-start.3 = (bf16[192,512]{1,0:T(8,128)(2,1)S(1)}, bf16[192,512]{1,0:T(8,128)(2,1)S(1)}, u32[]{:S(2)}, u32[]{:S(2)}) collective-permute-start(bf16[192,512]{1,0:T(8,128)(2,1)S(1)} %get-tuple-element.2), channel_id=1, source_target_pairs={{0,1},{1,2},{2,3},{3,0},{4,5},{5,6},{6,7},{7,4},{8,9},{9,10},{10,1... | collective-permute-start | bytes 589832 | tf_op jit(solution)/shard_map/ppermute | solution.py:33
  48.3 3.4 %collective-permute-start.4 = (bf16[192,512]{1,0:T(8,128)(2,1)S(1)}, bf16[192,512]{1,0:T(8,128)(2,1)S(1)}, u32[]{:S(2)}, u32[]{:S(2)}) collective-permute-start(bf16[192,512]{1,0:T(8,128)(2,1)S(1)} %get-tuple-element.4), channel_id=1, source_target_pairs={{0,3},{1,0},{2,1},{3,2},{4,7},{5,4},{6,5},{7,6},{8,11},{9,8},{10,9... | collective-permute-start | bytes 589832 | tf_op jit(solution)/shard_map/ppermute | solution.py:33
  51.7 3.4 %collective-permute-start.5 = (bf16[192,512]{1,0:T(8,128)(2,1)S(1)}, bf16[192,512]{1,0:T(8,128)(2,1)S(1)}, u32[]{:S(2)}, u32[]{:S(2)}) collective-permute-start(bf16[192,512]{1,0:T(8,128)(2,1)S(1)} %get-tuple-element.3), channel_id=1, source_target_pairs={{0,2},{1,3},{2,0},{3,1},{4,6},{5,7},{6,4},{7,5},{8,10},{9,11},{10,... | collective-permute-start | bytes 589832 | tf_op jit(solution)/shard_map/ppermute | solution.py:33
  56.0 4.6 %collective-permute-done.5 = bf16[192,512]{1,0:T(8,128)(2,1)S(1)} collective-permute-done((bf16[192,512]{1,0:T(8,128)(2,1)S(1)}, bf16[192,512]{1,0:T(8,128)(2,1)S(1)}, u32[]{:S(2)}, u32[]{:S(2)}) %collective-permute-start.5) | collective-permute-done | bytes 196640 | tf_op jit(solution)/shard_map/ppermute | solution.py:33
  61.7 3.5 %all-to-all-start.4 = ((bf16[4,8,24,512]{3,2,1,0:T(8,128)(2,1)}), bf16[4,8,24,512]{3,2,1,0:T(8,128)(2,1)S(1)}, u32[]{:S(2)}, u32[]{:S(2)}) async-start(bf16[4,8,24,512]{3,2,1,0:T(8,128)(2,1)} %broadcast_in_dim.16), calls=%async_computation.4 | async-start | bytes 1572864 | tf_op jit(solution)/shard_map/all_to_all | solution.py:19
  66.0 9.4 %all-to-all-done.4 = bf16[4,8,24,512]{3,2,1,0:T(8,128)(2,1)S(1)} async-done(((bf16[4,8,24,512]{3,2,1,0:T(8,128)(2,1)}), bf16[4,8,24,512]{3,2,1,0:T(8,128)(2,1)S(1)}, u32[]{:S(2)}, u32[]{:S(2)}) %all-to-all-start.4) | async-done | bytes 786464 | tf_op jit(solution)/shard_map/all_to_all | solution.py:19
  75.4 9.6 %all-to-all-start = ((bf16[8,32,512]{2,1,0:T(8,128)(2,1)}), bf16[8,32,512]{2,1,0:T(8,128)(2,1)S(1)}, u32[]{:S(2)}, u32[]{:S(2)}) async-start(bf16[8,32,512]{2,1,0:T(8,128)(2,1)} %pad_maximum_fusion), calls=%async_computation | async-start | bytes 524288 | tf_op jit(solution)/shard_map/all_to_all | solution.py:23
  85.0 1.2 fusion.3
  86.3 10.7 %all-to-all-done = bf16[8,32,512]{2,1,0:T(8,128)(2,1)S(1)} async-done(((bf16[8,32,512]{2,1,0:T(8,128)(2,1)}), bf16[8,32,512]{2,1,0:T(8,128)(2,1)S(1)}, u32[]{:S(2)}, u32[]{:S(2)}) %all-to-all-start) | async-done | bytes 262176 | tf_op jit(solution)/shard_map/all_to_all | solution.py:23
  96.9 9.2 %all-to-all-start.5 = ((f32[8,96,256]{2,1,0:T(8,128)}), f32[8,96,256]{2,1,0:T(8,128)S(1)}, u32[]{:S(2)}, u32[]{:S(2)}) async-start(f32[8,96,256]{2,1,0:T(8,128)} %fusion.3), calls=%async_computation.5 | async-start | bytes 1572864 | tf_op jit(solution)/shard_map/all_to_all | solution.py:23
  106.2 12.0 %all-to-all-done.5 = f32[8,96,256]{2,1,0:T(8,128)S(1)} async-done(((f32[8,96,256]{2,1,0:T(8,128)}), f32[8,96,256]{2,1,0:T(8,128)S(1)}, u32[]{:S(2)}, u32[]{:S(2)}) %all-to-all-start.5) | async-done | bytes 786464 | tf_op jit(solution)/shard_map/all_to_all | solution.py:23
  118.3 8.3 %collective-permute-start.6 = (f32[96,256]{1,0:T(8,128)S(1)}, f32[96,256]{1,0:T(8,128)S(1)}, u32[]{:S(2)}, u32[]{:S(2)}) collective-permute-start(f32[96,256]{1,0:T(8,128)S(1)} %reduce_sum.46), channel_id=1, source_target_pairs={{0,256},{256,0},{1,257},{257,1},{2,258},{258,2},{3,259},{259,3},{4... | collective-permute-start | bytes 294920 | tf_op jit(solution)/shard_map/ppermute | solution.py:171
  127.4 4.8 %all-to-all-start.1 = ((bf16[8,24,512]{2,1,0:T(8,128)(2,1)}), bf16[8,24,512]{2,1,0:T(8,128)(2,1)S(1)}, u32[]{:S(2)}, u32[]{:S(2)}) async-start(bf16[8,24,512]{2,1,0:T(8,128)(2,1)} %broadcast_in_dim.12), calls=%async_computation.1 | async-start | bytes 393216 | tf_op jit(solution)/shard_map/all_to_all | solution.py:19
  133.2 2.2 %collective-permute-start.7 = (bf16[1,96,256]{2,1,0:T(8,128)(2,1)S(1)}, bf16[1,96,256]{2,1,0:T(8,128)(2,1)S(1)}, u32[]{:S(2)}, u32[]{:S(2)}) collective-permute-start(bf16[1,96,256]{2,1,0:T(8,128)(2,1)S(1)} %fusion.6), channel_id=1, source_target_pairs={{0,64},{64,0},{128,192},{192,128},{1,65},{65,1},{129,193},{193,129... | collective-permute-start | bytes 147464 | tf_op jit(solution)/shard_map/ppermute | solution.py:37
  136.6 1.7 collective-permute-done.7
  138.3 2.8 %collective-permute-start.8 = (bf16[2,96,256]{2,1,0:T(8,128)(2,1)S(1)}, bf16[2,96,256]{2,1,0:T(8,128)(2,1)S(1)}, u32[]{:S(2)}, u32[]{:S(2)}) collective-permute-start(bf16[2,96,256]{2,1,0:T(8,128)(2,1)S(1)} %pad_maximum_fusion.4), channel_id=1, source_target_pairs={{0,192},{64,128},{128,64},{192,0},{1,193},{65,129},{129,65},{193,1... | collective-permute-start | bytes 294920 | tf_op jit(solution)/shard_map/ppermute | solution.py:37
  141.3 7.2 %all-to-all-done.1 = bf16[8,24,512]{2,1,0:T(8,128)(2,1)S(1)} async-done(((bf16[8,24,512]{2,1,0:T(8,128)(2,1)}), bf16[8,24,512]{2,1,0:T(8,128)(2,1)S(1)}, u32[]{:S(2)}, u32[]{:S(2)}) %all-to-all-start.1) | async-done | bytes 196640 | tf_op jit(solution)/shard_map/all_to_all | solution.py:19
  149.4 3.5 %all-to-all-start.2 = ((bf16[4,192,512]{2,1,0:T(8,128)(2,1)}), bf16[4,192,512]{2,1,0:T(8,128)(2,1)S(1)}, u32[]{:S(2)}, u32[]{:S(2)}) async-start(bf16[4,192,512]{2,1,0:T(8,128)(2,1)} %broadcast_in_dim.14), calls=%async_computation.2 | async-start | bytes 1572864 | tf_op jit(solution)/shard_map/all_to_all | solution.py:19
  153.0 2.8 %all-gather.1 = bf16[8,96,256]{2,1,0:T(8,128)(2,1)S(1)} all-gather(bf16[4,96,256]{2,1,0:T(8,128)(2,1)S(1)} %pad_maximum_fusion.2), channel_id=3, replica_groups=mesh['zh'=2,'y'=4,'c'=2,'zl'=8,'x'=4] {'c'}, dimensions={0}, use_global_device_ids=true | all-gather | bytes 589824 | tf_op jit(solution)/shard_map/all_gather | solution.py:175
  158.2 6.2 %all-to-all-done.2 = bf16[4,192,512]{2,1,0:T(8,128)(2,1)S(1)} async-done(((bf16[4,192,512]{2,1,0:T(8,128)(2,1)}), bf16[4,192,512]{2,1,0:T(8,128)(2,1)S(1)}, u32[]{:S(2)}, u32[]{:S(2)}) %all-to-all-start.2) | async-done | bytes 786464 | tf_op jit(solution)/shard_map/all_to_all | solution.py:19
  164.5 8.9 %partial_scores.1 = bf16[16,24,128]{2,1,0:T(8,128)(2,1)S(1)} custom-call(f32[1,256]{1,0:T(1,128)S(1)} %bitcast.50, f32[4,4,128,128]{3,2,1,0:T(8,128)S(1)} %fusion.table_ref, bf16[256,512]{1,0:T(8,128)(2,1)S(1)} %bitcast.48, bf16[512,512]{1,0:T(8,128)(2,1)S(1)} %bitcast.47, bf16[256,256]{1,0:T(8,128)(2,1)S(1)} %bitcast.49, f32[256,512]{1,0:T(8,128)S(1)} %bitcast.46, ...), custom_call_target="tpu_custom_call" | custom-call | tf_op jit(solution)/shard_map/partial_scores/pallas_call | solution.py:101
  173.3 20.5 %all_to_all.40 = bf16[16,24,128]{2,1,0:T(8,128)(2,1)S(1)} all-to-all(bf16[16,24,128]{2,1,0:T(8,128)(2,1)S(1)} %partial_scores.1), channel_id=1, replica_groups=mesh['zh'=2,'y'=4,'c'=2,'zl'=8,'x'=4] {'zh','zl'}, dimensions={0} | all-to-all | bytes 196608 | tf_op jit(solution)/shard_map/all_to_all | solution.py:23
  194.4 1.6 pack.1
  196.0 9.0 %all-to-all-start.7 = ((f32[32,8,128]{2,1,0:T(8,128)}), f32[32,8,128]{2,1,0:T(8,128)S(1)}, u32[]{:S(2)}, u32[]{:S(2)}) async-start(f32[32,8,128]{2,1,0:T(8,128)} %pack.1), calls=%async_computation.7 | async-start | bytes 262144 | tf_op jit(solution)/shard_map/all_to_all | solution.py:23
  205.2 7.5 %all-to-all-done.7 = f32[32,8,128]{2,1,0:T(8,128)S(1)} async-done(((f32[32,8,128]{2,1,0:T(8,128)}), f32[32,8,128]{2,1,0:T(8,128)S(1)}, u32[]{:S(2)}, u32[]{:S(2)}) %all-to-all-start.7) | async-done | bytes 131104 | tf_op jit(solution)/shard_map/all_to_all | solution.py:23
  (68 shorter events, 13.6 us)
Async XLA Ops:
  0.6 44.1 %copy-start = (bf16[256,512]{1,0:T(8,128)(2,1)S(1)}, bf16[256,512]{1,0:T(8,128)(2,1)}, u32[]{:S(2)}) copy-start(bf16[256,512]{1,0:T(8,128)(2,1)} %param.14) | copy-start | bytes 786436
  2.1 17.6 %collective-permute-start = (bf16[48,256]{1,0:T(8,128)(2,1)S(1)}, bf16[48,256]{1,0:T(8,128)(2,1)S(1)}, u32[]{:S(2)}, u32[]{:S(2)}) collective-permute-start(bf16[48,256]{1,0:T(8,128)(2,1)S(1)} %pad_maximum_fusion.6), channel_id=1, source_target_pairs={{0,256},{256,0},{1,257},{257,1},{2,258},{258,2},{3,259},{259,3},{4... | collective-permute-start | bytes 73736 | tf_op jit(solution)/shard_map/ppermute | solution.py:181
  19.7 4.8 %collective-permute-start.1 = (bf16[2,48,256]{2,1,0:T(8,128)(2,1)S(1)}, bf16[2,48,256]{2,1,0:T(8,128)(2,1)S(1)}, u32[]{:S(2)}, u32[]{:S(2)}) collective-permute-start(bf16[2,48,256]{2,1,0:T(8,128)(2,1)S(1)} %bitcast.65), channel_id=1, source_target_pairs={{0,64},{64,0},{128,192},{192,128},{1,65},{65,1},{129,193},{193,129... | collective-permute-start | bytes 147464 | tf_op jit(solution)/shard_map/ppermute | solution.py:37
  24.6 14.9 %collective-permute-start.2 = (bf16[4,48,256]{2,1,0:T(8,128)(2,1)S(1)}, bf16[4,48,256]{2,1,0:T(8,128)(2,1)S(1)}, u32[]{:S(2)}, u32[]{:S(2)}) collective-permute-start(bf16[4,48,256]{2,1,0:T(8,128)(2,1)S(1)} %pad_maximum_fusion.3), channel_id=1, source_target_pairs={{0,192},{64,128},{128,64},{192,0},{1,193},{65,129},{129,65},{193,1... | collective-permute-start | bytes 294920 | tf_op jit(solution)/shard_map/ppermute | solution.py:37
  30.6 30.1 %all-to-all-start.3 = ((bf16[8,24,512]{2,1,0:T(8,128)(2,1)}), bf16[8,24,512]{2,1,0:T(8,128)(2,1)S(1)}, u32[]{:S(2)}, u32[]{:S(2)}) async-start(bf16[8,24,512]{2,1,0:T(8,128)(2,1)} %broadcast_in_dim.15), calls=%async_computation.3 | async-start | bytes 393216 | tf_op jit(solution)/shard_map/all_to_all | solution.py:19
  45.2 10.0 %collective-permute-start.3 = (bf16[192,512]{1,0:T(8,128)(2,1)S(1)}, bf16[192,512]{1,0:T(8,128)(2,1)S(1)}, u32[]{:S(2)}, u32[]{:S(2)}) collective-permute-start(bf16[192,512]{1,0:T(8,128)(2,1)S(1)} %get-tuple-element.2), channel_id=1, source_target_pairs={{0,1},{1,2},{2,3},{3,0},{4,5},{5,6},{6,7},{7,4},{8,9},{9,10},{10,1... | collective-permute-start | bytes 589832 | tf_op jit(solution)/shard_map/ppermute | solution.py:33
  48.3 7.7 %collective-permute-start.4 = (bf16[192,512]{1,0:T(8,128)(2,1)S(1)}, bf16[192,512]{1,0:T(8,128)(2,1)S(1)}, u32[]{:S(2)}, u32[]{:S(2)}) collective-permute-start(bf16[192,512]{1,0:T(8,128)(2,1)S(1)} %get-tuple-element.4), channel_id=1, source_target_pairs={{0,3},{1,0},{2,1},{3,2},{4,7},{5,4},{6,5},{7,6},{8,11},{9,8},{10,9... | collective-permute-start | bytes 589832 | tf_op jit(solution)/shard_map/ppermute | solution.py:33
  51.7 8.9 %collective-permute-start.5 = (bf16[192,512]{1,0:T(8,128)(2,1)S(1)}, bf16[192,512]{1,0:T(8,128)(2,1)S(1)}, u32[]{:S(2)}, u32[]{:S(2)}) collective-permute-start(bf16[192,512]{1,0:T(8,128)(2,1)S(1)} %get-tuple-element.3), channel_id=1, source_target_pairs={{0,2},{1,3},{2,0},{3,1},{4,6},{5,7},{6,4},{7,5},{8,10},{9,11},{10,... | collective-permute-start | bytes 589832 | tf_op jit(solution)/shard_map/ppermute | solution.py:33
  61.7 13.7 %all-to-all-start.4 = ((bf16[4,8,24,512]{3,2,1,0:T(8,128)(2,1)}), bf16[4,8,24,512]{3,2,1,0:T(8,128)(2,1)S(1)}, u32[]{:S(2)}, u32[]{:S(2)}) async-start(bf16[4,8,24,512]{3,2,1,0:T(8,128)(2,1)} %broadcast_in_dim.16), calls=%async_computation.4 | async-start | bytes 1572864 | tf_op jit(solution)/shard_map/all_to_all | solution.py:19
  65.2 19.8 %copy-start.2 = (bf16[512,256]{1,0:T(8,128)(2,1)S(1)}, bf16[512,256]{1,0:T(8,128)(2,1)}, u32[]{:S(2)}) copy-start(bf16[512,256]{1,0:T(8,128)(2,1)} %param.15) | copy-start | bytes 786436
  75.4 21.5 %all-to-all-start = ((bf16[8,32,512]{2,1,0:T(8,128)(2,1)}), bf16[8,32,512]{2,1,0:T(8,128)(2,1)S(1)}, u32[]{:S(2)}, u32[]{:S(2)}) async-start(bf16[8,32,512]{2,1,0:T(8,128)(2,1)} %pad_maximum_fusion), calls=%async_computation | async-start | bytes 524288 | tf_op jit(solution)/shard_map/all_to_all | solution.py:23
  86.3 19.8 %copy-start.3 = (s32[512]{0:T(512)S(1)}, s32[512]{0:T(512)}, u32[]{:S(2)}) copy-start(s32[512]{0:T(512)} %param.19) | copy-start | bytes 6148
  96.9 21.4 %all-to-all-start.5 = ((f32[8,96,256]{2,1,0:T(8,128)}), f32[8,96,256]{2,1,0:T(8,128)S(1)}, u32[]{:S(2)}, u32[]{:S(2)}) async-start(f32[8,96,256]{2,1,0:T(8,128)} %fusion.3), calls=%async_computation.5 | async-start | bytes 1572864 | tf_op jit(solution)/shard_map/all_to_all | solution.py:23
  118.3 17.4 %copy-start.1 = (f32[512,256]{1,0:T(8,128)S(1)}, f32[512,256]{1,0:T(8,128)}, u32[]{:S(2)}) copy-start(f32[512,256]{1,0:T(8,128)} %param.16) | copy-start | bytes 1572868
  118.3 14.8 %collective-permute-start.6 = (f32[96,256]{1,0:T(8,128)S(1)}, f32[96,256]{1,0:T(8,128)S(1)}, u32[]{:S(2)}, u32[]{:S(2)}) collective-permute-start(f32[96,256]{1,0:T(8,128)S(1)} %reduce_sum.46), channel_id=1, source_target_pairs={{0,256},{256,0},{1,257},{257,1},{2,258},{258,2},{3,259},{259,3},{4... | collective-permute-start | bytes 294920 | tf_op jit(solution)/shard_map/ppermute | solution.py:171
  127.4 21.1 %all-to-all-start.1 = ((bf16[8,24,512]{2,1,0:T(8,128)(2,1)}), bf16[8,24,512]{2,1,0:T(8,128)(2,1)S(1)}, u32[]{:S(2)}, u32[]{:S(2)}) async-start(bf16[8,24,512]{2,1,0:T(8,128)(2,1)} %broadcast_in_dim.12), calls=%async_computation.1 | async-start | bytes 393216 | tf_op jit(solution)/shard_map/all_to_all | solution.py:19
  133.2 5.1 %collective-permute-start.7 = (bf16[1,96,256]{2,1,0:T(8,128)(2,1)S(1)}, bf16[1,96,256]{2,1,0:T(8,128)(2,1)S(1)}, u32[]{:S(2)}, u32[]{:S(2)}) collective-permute-start(bf16[1,96,256]{2,1,0:T(8,128)(2,1)S(1)} %fusion.6), channel_id=1, source_target_pairs={{0,64},{64,0},{128,192},{192,128},{1,65},{65,1},{129,193},{193,129... | collective-permute-start | bytes 147464 | tf_op jit(solution)/shard_map/ppermute | solution.py:37
  135.7 5.5 %copy-start.4 = (s32[256]{0:T(256)S(1)}, s32[256]{0:T(256)}, u32[]{:S(2)}) copy-start(s32[256]{0:T(256)} %param.18) | copy-start | bytes 3076
  138.3 14.6 %collective-permute-start.8 = (bf16[2,96,256]{2,1,0:T(8,128)(2,1)S(1)}, bf16[2,96,256]{2,1,0:T(8,128)(2,1)S(1)}, u32[]{:S(2)}, u32[]{:S(2)}) collective-permute-start(bf16[2,96,256]{2,1,0:T(8,128)(2,1)S(1)} %pad_maximum_fusion.4), channel_id=1, source_target_pairs={{0,192},{64,128},{128,64},{192,0},{1,193},{65,129},{129,65},{193,1... | collective-permute-start | bytes 294920 | tf_op jit(solution)/shard_map/ppermute | solution.py:37
  149.4 14.9 %all-to-all-start.2 = ((bf16[4,192,512]{2,1,0:T(8,128)(2,1)}), bf16[4,192,512]{2,1,0:T(8,128)(2,1)S(1)}, u32[]{:S(2)}, u32[]{:S(2)}) async-start(bf16[4,192,512]{2,1,0:T(8,128)(2,1)} %broadcast_in_dim.14), calls=%async_computation.2 | async-start | bytes 1572864 | tf_op jit(solution)/shard_map/all_to_all | solution.py:19
  196.0 16.7 %all-to-all-start.7 = ((f32[32,8,128]{2,1,0:T(8,128)}), f32[32,8,128]{2,1,0:T(8,128)S(1)}, u32[]{:S(2)}, u32[]{:S(2)}) async-start(f32[32,8,128]{2,1,0:T(8,128)} %pack.1), calls=%async_computation.7 | async-start | bytes 262144 | tf_op jit(solution)/shard_map/all_to_all | solution.py:23

commit v4 on v3

--- a/solution.py
+++ b/solution.py
@@ -82,6 +82,8 @@
                 precision=lax.Precision.HIGHEST,
                 preferred_element_type=f32,
             )
+    rest = pltpu.roll(docs - docs.astype(bf16).astype(f32), 64, 1)
+    docs = jnp.where(lax.broadcasted_iota(jnp.int32, docs.shape, 1) < 64, docs, rest)
     half = S // 2
     low = lax.broadcasted_iota(jnp.int32, (half, 128), 1) < 64
     for m in range(sum_ref.shape[1] // 128):
@@ -115,7 +117,9 @@
 def pack_kernel(total_ref, out_ref):
     half = S // 2
     rows = total_ref.shape[0]
-    total = jnp.concatenate([total_ref[...], jnp.zeros((128 - rows, 128), jnp.float32)], axis=0)
+    docs = total_ref[half:, :] + pltpu.roll(total_ref[half:, :], 64, 1)
+    empty = jnp.zeros((128 - rows, 128), jnp.float32)
+    total = jnp.concatenate([total_ref[:half, :], docs, empty], axis=0)
     turned = jnp.transpose(total)
     lane = lax.broadcasted_iota(jnp.int32, (DOCS, 128), 1)
     docs = jnp.zeros((DOCS, 128), jnp.float32)

time: 215 us -> 215 us (level)
  no operation moved by 1% of the time
where the time goes in v4:
time: 215 us; the launch traced here: 214 us
  starting transfers between devices  95.7 us (45%)
  waiting for transfers between devices  64 us (30%)
  blocking collectives  28.6 us (13%)
  Pallas kernels  10.6 us (5%)
  local copies, waits for them, and re-layouts  7.46 us (3%)
  other arithmetic  3.9 us (2%)
    all_to_all x3, waiting for transfers between devices, exchange(): return lax.all_to_all(parts, axes, 0, 0, tiled=True)  30.2 us
    all_to_all x3, starting transfers between devices, exchange(): return lax.all_to_all(parts, axes, 0, 0, tiled=True)  27.8 us
    all_to_all x4, waiting for transfers between devices, spread(): lax.all_to_all(jnp.broadcast_to(v[None], (n,) + v.shape), axes, 0, 0, til...  22.8 us
    all_to_all x4, starting transfers between devices, spread(): lax.all_to_all(jnp.broadcast_to(v[None], (n,) + v.shape), axes, 0, 0, til...  20.6 us
    all_to_all x1, blocking collectives, exchange(): return lax.all_to_all(parts, axes, 0, 0, tiled=True)  20.5 us
    ppermute x1, starting transfers between devices, body(): other = lax.ppermute(g, 'zh', [(0, 1), (1, 0)])  16.2 us
    ppermute x4, starting transfers between devices, meet(): other = lax.ppermute(v, axis, list(enumerate(partner)))  12.8 us
    ppermute x3, starting transfers between devices, shift(): return lax.ppermute(v, axis, [(i, (i + k) % n) for i in range(n)])  9.94 us
  transfers between devices with their start and end apart: 16, of which 12 were waited for; matrix products, arithmetic and copies ran while one was open for 4% of the time, Pallas kernels for 0%

profile of v4, /device:TPU:1, one launch (start us, length us, event | category | flops | bytes accessed | tf_op | source)
XLA Modules:
  0.0 213.6 jit_solution(566126347531539197)
XLA Ops:
  2.1 16.2 %collective-permute-start = (bf16[48,256]{1,0:T(8,128)(2,1)S(1)}, bf16[48,256]{1,0:T(8,128)(2,1)S(1)}, u32[]{:S(2)}, u32[]{:S(2)}) collective-permute-start(bf16[48,256]{1,0:T(8,128)(2,1)S(1)} %pad_maximum_fusion.6), channel_id=1, source_target_pairs={{0,256},{256,0},{1,257},{257,1},{2,258},{258,2},{3,259},{259,3},{4... | collective-permute-start | bytes 73736 | tf_op jit(solution)/shard_map/ppermute | solution.py:185
  18.4 1.3 collective-permute-done
  19.7 3.2 %collective-permute-start.1 = (bf16[2,48,256]{2,1,0:T(8,128)(2,1)S(1)}, bf16[2,48,256]{2,1,0:T(8,128)(2,1)S(1)}, u32[]{:S(2)}, u32[]{:S(2)}) collective-permute-start(bf16[2,48,256]{2,1,0:T(8,128)(2,1)S(1)} %bitcast.65), channel_id=1, source_target_pairs={{0,64},{64,0},{128,192},{192,128},{1,65},{65,1},{129,193},{193,129... | collective-permute-start | bytes 147464 | tf_op jit(solution)/shard_map/ppermute | solution.py:37
  22.9 1.6 collective-permute-done.1
  24.6 4.6 %collective-permute-start.2 = (bf16[4,48,256]{2,1,0:T(8,128)(2,1)S(1)}, bf16[4,48,256]{2,1,0:T(8,128)(2,1)S(1)}, u32[]{:S(2)}, u32[]{:S(2)}) collective-permute-start(bf16[4,48,256]{2,1,0:T(8,128)(2,1)S(1)} %pad_maximum_fusion.3), channel_id=1, source_target_pairs={{0,192},{64,128},{128,64},{192,0},{1,193},{65,129},{129,65},{193,1... | collective-permute-start | bytes 294920 | tf_op jit(solution)/shard_map/ppermute | solution.py:37
  30.6 8.8 %all-to-all-start.3 = ((bf16[8,24,512]{2,1,0:T(8,128)(2,1)}), bf16[8,24,512]{2,1,0:T(8,128)(2,1)S(1)}, u32[]{:S(2)}, u32[]{:S(2)}) async-start(bf16[8,24,512]{2,1,0:T(8,128)(2,1)} %broadcast_in_dim.15), calls=%async_computation.3 | async-start | bytes 393216 | tf_op jit(solution)/shard_map/all_to_all | solution.py:19
  39.5 5.2 %all-gather = bf16[16,48,256]{2,1,0:T(8,128)(2,1)S(1)} all-gather(bf16[8,48,256]{2,1,0:T(8,128)(2,1)S(1)} %pad_maximum_fusion.1), channel_id=2, replica_groups=mesh['zh'=2,'y'=4,'c'=2,'zl'=8,'x'=4] {'c'}, dimensions={0}, use_global_device_ids=true | all-gather | bytes 589824 | tf_op jit(solution)/shard_map/all_gather | solution.py:191
  45.2 3.1 %collective-permute-start.3 = (bf16[192,512]{1,0:T(8,128)(2,1)S(1)}, bf16[192,512]{1,0:T(8,128)(2,1)S(1)}, u32[]{:S(2)}, u32[]{:S(2)}) collective-permute-start(bf16[192,512]{1,0:T(8,128)(2,1)S(1)} %get-tuple-element.2), channel_id=1, source_target_pairs={{0,1},{1,2},{2,3},{3,0},{4,5},{5,6},{6,7},{7,4},{8,9},{9,10},{10,1... | collective-permute-start | bytes 589832 | tf_op jit(solution)/shard_map/ppermute | solution.py:33
  48.3 3.4 %collective-permute-start.4 = (bf16[192,512]{1,0:T(8,128)(2,1)S(1)}, bf16[192,512]{1,0:T(8,128)(2,1)S(1)}, u32[]{:S(2)}, u32[]{:S(2)}) collective-permute-start(bf16[192,512]{1,0:T(8,128)(2,1)S(1)} %get-tuple-element.4), channel_id=1, source_target_pairs={{0,3},{1,0},{2,1},{3,2},{4,7},{5,4},{6,5},{7,6},{8,11},{9,8},{10,9... | collective-permute-start | bytes 589832 | tf_op jit(solution)/shard_map/ppermute | solution.py:33
  51.7 3.4 %collective-permute-start.5 = (bf16[192,512]{1,0:T(8,128)(2,1)S(1)}, bf16[192,512]{1,0:T(8,128)(2,1)S(1)}, u32[]{:S(2)}, u32[]{:S(2)}) collective-permute-start(bf16[192,512]{1,0:T(8,128)(2,1)S(1)} %get-tuple-element.3), channel_id=1, source_target_pairs={{0,2},{1,3},{2,0},{3,1},{4,6},{5,7},{6,4},{7,5},{8,10},{9,11},{10,... | collective-permute-start | bytes 589832 | tf_op jit(solution)/shard_map/ppermute | solution.py:33
  56.0 4.6 %collective-permute-done.5 = bf16[192,512]{1,0:T(8,128)(2,1)S(1)} collective-permute-done((bf16[192,512]{1,0:T(8,128)(2,1)S(1)}, bf16[192,512]{1,0:T(8,128)(2,1)S(1)}, u32[]{:S(2)}, u32[]{:S(2)}) %collective-permute-start.5) | collective-permute-done | bytes 196640 | tf_op jit(solution)/shard_map/ppermute | solution.py:33
  61.7 3.5 %all-to-all-start.4 = ((bf16[4,8,24,512]{3,2,1,0:T(8,128)(2,1)}), bf16[4,8,24,512]{3,2,1,0:T(8,128)(2,1)S(1)}, u32[]{:S(2)}, u32[]{:S(2)}) async-start(bf16[4,8,24,512]{3,2,1,0:T(8,128)(2,1)} %broadcast_in_dim.16), calls=%async_computation.4 | async-start | bytes 1572864 | tf_op jit(solution)/shard_map/all_to_all | solution.py:19
  66.0 9.4 %all-to-all-done.4 = bf16[4,8,24,512]{3,2,1,0:T(8,128)(2,1)S(1)} async-done(((bf16[4,8,24,512]{3,2,1,0:T(8,128)(2,1)}), bf16[4,8,24,512]{3,2,1,0:T(8,128)(2,1)S(1)}, u32[]{:S(2)}, u32[]{:S(2)}) %all-to-all-start.4) | async-done | bytes 786464 | tf_op jit(solution)/shard_map/all_to_all | solution.py:19
  75.4 9.6 %all-to-all-start = ((bf16[8,32,512]{2,1,0:T(8,128)(2,1)}), bf16[8,32,512]{2,1,0:T(8,128)(2,1)S(1)}, u32[]{:S(2)}, u32[]{:S(2)}) async-start(bf16[8,32,512]{2,1,0:T(8,128)(2,1)} %pad_maximum_fusion), calls=%async_computation | async-start | bytes 524288 | tf_op jit(solution)/shard_map/all_to_all | solution.py:23
  85.0 1.2 fusion.3
  86.3 10.7 %all-to-all-done = bf16[8,32,512]{2,1,0:T(8,128)(2,1)S(1)} async-done(((bf16[8,32,512]{2,1,0:T(8,128)(2,1)}), bf16[8,32,512]{2,1,0:T(8,128)(2,1)S(1)}, u32[]{:S(2)}, u32[]{:S(2)}) %all-to-all-start) | async-done | bytes 262176 | tf_op jit(solution)/shard_map/all_to_all | solution.py:23
  96.9 9.2 %all-to-all-start.5 = ((f32[8,96,256]{2,1,0:T(8,128)}), f32[8,96,256]{2,1,0:T(8,128)S(1)}, u32[]{:S(2)}, u32[]{:S(2)}) async-start(f32[8,96,256]{2,1,0:T(8,128)} %fusion.3), calls=%async_computation.5 | async-start | bytes 1572864 | tf_op jit(solution)/shard_map/all_to_all | solution.py:23
  106.2 12.0 %all-to-all-done.5 = f32[8,96,256]{2,1,0:T(8,128)S(1)} async-done(((f32[8,96,256]{2,1,0:T(8,128)}), f32[8,96,256]{2,1,0:T(8,128)S(1)}, u32[]{:S(2)}, u32[]{:S(2)}) %all-to-all-start.5) | async-done | bytes 786464 | tf_op jit(solution)/shard_map/all_to_all | solution.py:23
  118.3 8.3 %collective-permute-start.6 = (f32[96,256]{1,0:T(8,128)S(1)}, f32[96,256]{1,0:T(8,128)S(1)}, u32[]{:S(2)}, u32[]{:S(2)}) collective-permute-start(f32[96,256]{1,0:T(8,128)S(1)} %reduce_sum.46), channel_id=1, source_target_pairs={{0,256},{256,0},{1,257},{257,1},{2,258},{258,2},{3,259},{259,3},{4... | collective-permute-start | bytes 294920 | tf_op jit(solution)/shard_map/ppermute | solution.py:175
  127.4 4.8 %all-to-all-start.1 = ((bf16[8,24,512]{2,1,0:T(8,128)(2,1)}), bf16[8,24,512]{2,1,0:T(8,128)(2,1)S(1)}, u32[]{:S(2)}, u32[]{:S(2)}) async-start(bf16[8,24,512]{2,1,0:T(8,128)(2,1)} %broadcast_in_dim.12), calls=%async_computation.1 | async-start | bytes 393216 | tf_op jit(solution)/shard_map/all_to_all | solution.py:19
  133.2 2.2 %collective-permute-start.7 = (bf16[1,96,256]{2,1,0:T(8,128)(2,1)S(1)}, bf16[1,96,256]{2,1,0:T(8,128)(2,1)S(1)}, u32[]{:S(2)}, u32[]{:S(2)}) collective-permute-start(bf16[1,96,256]{2,1,0:T(8,128)(2,1)S(1)} %fusion.6), channel_id=1, source_target_pairs={{0,64},{64,0},{128,192},{192,128},{1,65},{65,1},{129,193},{193,129... | collective-permute-start | bytes 147464 | tf_op jit(solution)/shard_map/ppermute | solution.py:37
  136.6 1.7 collective-permute-done.7
  138.3 2.8 %collective-permute-start.8 = (bf16[2,96,256]{2,1,0:T(8,128)(2,1)S(1)}, bf16[2,96,256]{2,1,0:T(8,128)(2,1)S(1)}, u32[]{:S(2)}, u32[]{:S(2)}) collective-permute-start(bf16[2,96,256]{2,1,0:T(8,128)(2,1)S(1)} %pad_maximum_fusion.4), channel_id=1, source_target_pairs={{0,192},{64,128},{128,64},{192,0},{1,193},{65,129},{129,65},{193,1... | collective-permute-start | bytes 294920 | tf_op jit(solution)/shard_map/ppermute | solution.py:37
  141.3 7.2 %all-to-all-done.1 = bf16[8,24,512]{2,1,0:T(8,128)(2,1)S(1)} async-done(((bf16[8,24,512]{2,1,0:T(8,128)(2,1)}), bf16[8,24,512]{2,1,0:T(8,128)(2,1)S(1)}, u32[]{:S(2)}, u32[]{:S(2)}) %all-to-all-start.1) | async-done | bytes 196640 | tf_op jit(solution)/shard_map/all_to_all | solution.py:19
  149.4 3.5 %all-to-all-start.2 = ((bf16[4,192,512]{2,1,0:T(8,128)(2,1)}), bf16[4,192,512]{2,1,0:T(8,128)(2,1)S(1)}, u32[]{:S(2)}, u32[]{:S(2)}) async-start(bf16[4,192,512]{2,1,0:T(8,128)(2,1)} %broadcast_in_dim.14), calls=%async_computation.2 | async-start | bytes 1572864 | tf_op jit(solution)/shard_map/all_to_all | solution.py:19
  153.0 2.8 %all-gather.1 = bf16[8,96,256]{2,1,0:T(8,128)(2,1)S(1)} all-gather(bf16[4,96,256]{2,1,0:T(8,128)(2,1)S(1)} %pad_maximum_fusion.2), channel_id=3, replica_groups=mesh['zh'=2,'y'=4,'c'=2,'zl'=8,'x'=4] {'c'}, dimensions={0}, use_global_device_ids=true | all-gather | bytes 589824 | tf_op jit(solution)/shard_map/all_gather | solution.py:179
  158.2 6.2 %all-to-all-done.2 = bf16[4,192,512]{2,1,0:T(8,128)(2,1)S(1)} async-done(((bf16[4,192,512]{2,1,0:T(8,128)(2,1)}), bf16[4,192,512]{2,1,0:T(8,128)(2,1)S(1)}, u32[]{:S(2)}, u32[]{:S(2)}) %all-to-all-start.2) | async-done | bytes 786464 | tf_op jit(solution)/shard_map/all_to_all | solution.py:19
  164.5 8.9 %partial_scores.1 = bf16[16,24,128]{2,1,0:T(8,128)(2,1)S(1)} custom-call(f32[1,256]{1,0:T(1,128)S(1)} %bitcast.50, f32[4,4,128,128]{3,2,1,0:T(8,128)S(1)} %fusion.table_ref, bf16[256,512]{1,0:T(8,128)(2,1)S(1)} %bitcast.48, bf16[512,512]{1,0:T(8,128)(2,1)S(1)} %bitcast.47, bf16[256,256]{1,0:T(8,128)(2,1)S(1)} %bitcast.49, f32[256,512]{1,0:T(8,128)S(1)} %bitcast.46, ...), custom_call_target="tpu_custom_call" | custom-call | tf_op jit(solution)/shard_map/partial_scores/pallas_call | solution.py:103
  173.4 20.5 %all_to_all.40 = bf16[16,24,128]{2,1,0:T(8,128)(2,1)S(1)} all-to-all(bf16[16,24,128]{2,1,0:T(8,128)(2,1)S(1)} %partial_scores.1), channel_id=1, replica_groups=mesh['zh'=2,'y'=4,'c'=2,'zl'=8,'x'=4] {'zh','zl'}, dimensions={0} | all-to-all | bytes 196608 | tf_op jit(solution)/shard_map/all_to_all | solution.py:23
  194.5 1.6 pack.1
  196.1 9.0 %all-to-all-start.7 = ((f32[32,8,128]{2,1,0:T(8,128)}), f32[32,8,128]{2,1,0:T(8,128)S(1)}, u32[]{:S(2)}, u32[]{:S(2)}) async-start(f32[32,8,128]{2,1,0:T(8,128)} %pack.1), calls=%async_computation.7 | async-start | bytes 262144 | tf_op jit(solution)/shard_map/all_to_all | solution.py:23
  205.3 7.5 %all-to-all-done.7 = f32[32,8,128]{2,1,0:T(8,128)S(1)} async-done(((f32[32,8,128]{2,1,0:T(8,128)}), f32[32,8,128]{2,1,0:T(8,128)S(1)}, u32[]{:S(2)}, u32[]{:S(2)}) %all-to-all-start.7) | async-done | bytes 131104 | tf_op jit(solution)/shard_map/all_to_all | solution.py:23
  (68 shorter events, 13.6 us)
Async XLA Ops:
  0.6 44.1 %copy-start = (bf16[256,512]{1,0:T(8,128)(2,1)S(1)}, bf16[256,512]{1,0:T(8,128)(2,1)}, u32[]{:S(2)}) copy-start(bf16[256,512]{1,0:T(8,128)(2,1)} %param.14) | copy-start | bytes 786436
  2.1 17.6 %collective-permute-start = (bf16[48,256]{1,0:T(8,128)(2,1)S(1)}, bf16[48,256]{1,0:T(8,128)(2,1)S(1)}, u32[]{:S(2)}, u32[]{:S(2)}) collective-permute-start(bf16[48,256]{1,0:T(8,128)(2,1)S(1)} %pad_maximum_fusion.6), channel_id=1, source_target_pairs={{0,256},{256,0},{1,257},{257,1},{2,258},{258,2},{3,259},{259,3},{4... | collective-permute-start | bytes 73736 | tf_op jit(solution)/shard_map/ppermute | solution.py:185
  19.7 4.8 %collective-permute-start.1 = (bf16[2,48,256]{2,1,0:T(8,128)(2,1)S(1)}, bf16[2,48,256]{2,1,0:T(8,128)(2,1)S(1)}, u32[]{:S(2)}, u32[]{:S(2)}) collective-permute-start(bf16[2,48,256]{2,1,0:T(8,128)(2,1)S(1)} %bitcast.65), channel_id=1, source_target_pairs={{0,64},{64,0},{128,192},{192,128},{1,65},{65,1},{129,193},{193,129... | collective-permute-start | bytes 147464 | tf_op jit(solution)/shard_map/ppermute | solution.py:37
  24.6 14.9 %collective-permute-start.2 = (bf16[4,48,256]{2,1,0:T(8,128)(2,1)S(1)}, bf16[4,48,256]{2,1,0:T(8,128)(2,1)S(1)}, u32[]{:S(2)}, u32[]{:S(2)}) collective-permute-start(bf16[4,48,256]{2,1,0:T(8,128)(2,1)S(1)} %pad_maximum_fusion.3), channel_id=1, source_target_pairs={{0,192},{64,128},{128,64},{192,0},{1,193},{65,129},{129,65},{193,1... | collective-permute-start | bytes 294920 | tf_op jit(solution)/shard_map/ppermute | solution.py:37
  30.6 30.1 %all-to-all-start.3 = ((bf16[8,24,512]{2,1,0:T(8,128)(2,1)}), bf16[8,24,512]{2,1,0:T(8,128)(2,1)S(1)}, u32[]{:S(2)}, u32[]{:S(2)}) async-start(bf16[8,24,512]{2,1,0:T(8,128)(2,1)} %broadcast_in_dim.15), calls=%async_computation.3 | async-start | bytes 393216 | tf_op jit(solution)/shard_map/all_to_all | solution.py:19
  45.2 10.0 %collective-permute-start.3 = (bf16[192,512]{1,0:T(8,128)(2,1)S(1)}, bf16[192,512]{1,0:T(8,128)(2,1)S(1)}, u32[]{:S(2)}, u32[]{:S(2)}) collective-permute-start(bf16[192,512]{1,0:T(8,128)(2,1)S(1)} %get-tuple-element.2), channel_id=1, source_target_pairs={{0,1},{1,2},{2,3},{3,0},{4,5},{5,6},{6,7},{7,4},{8,9},{9,10},{10,1... | collective-permute-start | bytes 589832 | tf_op jit(solution)/shard_map/ppermute | solution.py:33
  48.3 7.7 %collective-permute-start.4 = (bf16[192,512]{1,0:T(8,128)(2,1)S(1)}, bf16[192,512]{1,0:T(8,128)(2,1)S(1)}, u32[]{:S(2)}, u32[]{:S(2)}) collective-permute-start(bf16[192,512]{1,0:T(8,128)(2,1)S(1)} %get-tuple-element.4), channel_id=1, source_target_pairs={{0,3},{1,0},{2,1},{3,2},{4,7},{5,4},{6,5},{7,6},{8,11},{9,8},{10,9... | collective-permute-start | bytes 589832 | tf_op jit(solution)/shard_map/ppermute | solution.py:33
  51.7 8.9 %collective-permute-start.5 = (bf16[192,512]{1,0:T(8,128)(2,1)S(1)}, bf16[192,512]{1,0:T(8,128)(2,1)S(1)}, u32[]{:S(2)}, u32[]{:S(2)}) collective-permute-start(bf16[192,512]{1,0:T(8,128)(2,1)S(1)} %get-tuple-element.3), channel_id=1, source_target_pairs={{0,2},{1,3},{2,0},{3,1},{4,6},{5,7},{6,4},{7,5},{8,10},{9,11},{10,... | collective-permute-start | bytes 589832 | tf_op jit(solution)/shard_map/ppermute | solution.py:33
  61.7 13.7 %all-to-all-start.4 = ((bf16[4,8,24,512]{3,2,1,0:T(8,128)(2,1)}), bf16[4,8,24,512]{3,2,1,0:T(8,128)(2,1)S(1)}, u32[]{:S(2)}, u32[]{:S(2)}) async-start(bf16[4,8,24,512]{3,2,1,0:T(8,128)(2,1)} %broadcast_in_dim.16), calls=%async_computation.4 | async-start | bytes 1572864 | tf_op jit(solution)/shard_map/all_to_all | solution.py:19
  65.2 19.8 %copy-start.2 = (bf16[512,256]{1,0:T(8,128)(2,1)S(1)}, bf16[512,256]{1,0:T(8,128)(2,1)}, u32[]{:S(2)}) copy-start(bf16[512,256]{1,0:T(8,128)(2,1)} %param.15) | copy-start | bytes 786436
  75.4 21.5 %all-to-all-start = ((bf16[8,32,512]{2,1,0:T(8,128)(2,1)}), bf16[8,32,512]{2,1,0:T(8,128)(2,1)S(1)}, u32[]{:S(2)}, u32[]{:S(2)}) async-start(bf16[8,32,512]{2,1,0:T(8,128)(2,1)} %pad_maximum_fusion), calls=%async_computation | async-start | bytes 524288 | tf_op jit(solution)/shard_map/all_to_all | solution.py:23
  86.3 19.8 %copy-start.3 = (s32[512]{0:T(512)S(1)}, s32[512]{0:T(512)}, u32[]{:S(2)}) copy-start(s32[512]{0:T(512)} %param.19) | copy-start | bytes 6148
  96.9 21.4 %all-to-all-start.5 = ((f32[8,96,256]{2,1,0:T(8,128)}), f32[8,96,256]{2,1,0:T(8,128)S(1)}, u32[]{:S(2)}, u32[]{:S(2)}) async-start(f32[8,96,256]{2,1,0:T(8,128)} %fusion.3), calls=%async_computation.5 | async-start | bytes 1572864 | tf_op jit(solution)/shard_map/all_to_all | solution.py:23
  118.3 17.4 %copy-start.1 = (f32[512,256]{1,0:T(8,128)S(1)}, f32[512,256]{1,0:T(8,128)}, u32[]{:S(2)}) copy-start(f32[512,256]{1,0:T(8,128)} %param.16) | copy-start | bytes 1572868
  118.3 14.8 %collective-permute-start.6 = (f32[96,256]{1,0:T(8,128)S(1)}, f32[96,256]{1,0:T(8,128)S(1)}, u32[]{:S(2)}, u32[]{:S(2)}) collective-permute-start(f32[96,256]{1,0:T(8,128)S(1)} %reduce_sum.46), channel_id=1, source_target_pairs={{0,256},{256,0},{1,257},{257,1},{2,258},{258,2},{3,259},{259,3},{4... | collective-permute-start | bytes 294920 | tf_op jit(solution)/shard_map/ppermute | solution.py:175
  127.4 21.1 %all-to-all-start.1 = ((bf16[8,24,512]{2,1,0:T(8,128)(2,1)}), bf16[8,24,512]{2,1,0:T(8,128)(2,1)S(1)}, u32[]{:S(2)}, u32[]{:S(2)}) async-start(bf16[8,24,512]{2,1,0:T(8,128)(2,1)} %broadcast_in_dim.12), calls=%async_computation.1 | async-start | bytes 393216 | tf_op jit(solution)/shard_map/all_to_all | solution.py:19
  133.2 5.1 %collective-permute-start.7 = (bf16[1,96,256]{2,1,0:T(8,128)(2,1)S(1)}, bf16[1,96,256]{2,1,0:T(8,128)(2,1)S(1)}, u32[]{:S(2)}, u32[]{:S(2)}) collective-permute-start(bf16[1,96,256]{2,1,0:T(8,128)(2,1)S(1)} %fusion.6), channel_id=1, source_target_pairs={{0,64},{64,0},{128,192},{192,128},{1,65},{65,1},{129,193},{193,129... | collective-permute-start | bytes 147464 | tf_op jit(solution)/shard_map/ppermute | solution.py:37
  135.7 5.5 %copy-start.4 = (s32[256]{0:T(256)S(1)}, s32[256]{0:T(256)}, u32[]{:S(2)}) copy-start(s32[256]{0:T(256)} %param.18) | copy-start | bytes 3076
  138.3 14.6 %collective-permute-start.8 = (bf16[2,96,256]{2,1,0:T(8,128)(2,1)S(1)}, bf16[2,96,256]{2,1,0:T(8,128)(2,1)S(1)}, u32[]{:S(2)}, u32[]{:S(2)}) collective-permute-start(bf16[2,96,256]{2,1,0:T(8,128)(2,1)S(1)} %pad_maximum_fusion.4), channel_id=1, source_target_pairs={{0,192},{64,128},{128,64},{192,0},{1,193},{65,129},{129,65},{193,1... | collective-permute-start | bytes 294920 | tf_op jit(solution)/shard_map/ppermute | solution.py:37
  149.4 14.9 %all-to-all-start.2 = ((bf16[4,192,512]{2,1,0:T(8,128)(2,1)}), bf16[4,192,512]{2,1,0:T(8,128)(2,1)S(1)}, u32[]{:S(2)}, u32[]{:S(2)}) async-start(bf16[4,192,512]{2,1,0:T(8,128)(2,1)} %broadcast_in_dim.14), calls=%async_computation.2 | async-start | bytes 1572864 | tf_op jit(solution)/shard_map/all_to_all | solution.py:19
  196.1 16.7 %all-to-all-start.7 = ((f32[32,8,128]{2,1,0:T(8,128)}), f32[32,8,128]{2,1,0:T(8,128)S(1)}, u32[]{:S(2)}, u32[]{:S(2)}) async-start(f32[32,8,128]{2,1,0:T(8,128)} %pack.1), calls=%async_computation.7 | async-start | bytes 262144 | tf_op jit(solution)/shard_map/all_to_all | solution.py:23
